TPU v7x, 256 devices: a whole 4x4x8 slice. The times are simulated.
256 devices in a mesh: seq: 16 (over z_lo, x, core), exp: 16 (over y, z_hi).
Axes of the slice: x: 4, y: 4, z: 8 (z_hi: 4, z_lo: 2; z = z_hi * 2 + z_lo), core: 2. Of those that a mesh axis runs over, the one named last changes fastest.
Arguments:
- tokens: bfloat16 [2, 16, 2048, 1024], P(None, 'exp', 'seq'), may hold values from -3 to 3
- queries: bfloat16 [2, 16, 2048, 1024], P(None, 'exp', 'seq'), may hold values from -6 to 6
- key_rows: bfloat16 [2, 16, 2048, 1024], P(None, 'exp', 'seq'), may hold values from -6 to 6
- value_rows: bfloat16 [2, 16, 2048, 1024], P(None, 'exp', 'seq'), may hold values from -6 to 6
- segments: int32 [2, 16, 2048], P(None, 'exp', 'seq'), may hold values from 0 to 3, never falling along the last dimension, each value on 1 to 1024 neighbouring positions
- bias_table: float32 [16, 32], replicated, may hold values from -3 to 5
- out_proj: bfloat16 [1024, 1024], replicated, may hold values from -0.75 to 0.75
- router: bfloat16 [1024, 16], replicated, may hold values from -0.1875 to 0.1875
- gate_weight: bfloat16 [16, 1024, 1408], P('exp'), may hold values from -0.1875 to 0.1875
- up_weight: bfloat16 [16, 1024, 1408], P('exp'), may hold values from -0.1875 to 0.1875
- down_weight: bfloat16 [16, 1408, 1024], P('exp'), may hold values from -0.15625 to 0.15625
- old_table: int32 [16], replicated, may hold values from 0 to 15, each once
- new_table: int32 [16], replicated, may hold values from 0 to 15, as said below
- routes_one: int32 [16, 2048, 2], P('exp', 'seq'), may hold values from 0 to 15, all different within a row; in each aligned block of 128 rows (0 to 127, 128 to 255, ..., all dimensions but the last counted through in order) at most 20 rows name the same one
- routes_two: int32 [16, 2048, 2], P('exp', 'seq'), may hold values from 0 to 15, all different within a row; in each aligned block of 128 rows (0 to 127, 128 to 255, ..., all dimensions but the last counted through in order) at most 20 rows name the same one
Outputs:
- layer_out: bfloat16 [2, 16, 2048, 1024], P(None, 'exp', 'seq')
Inputs may be any that keep to these rules, and one draw needn't show every extreme that they name: `old_table`: each position holds a different expert. `new_table`: no expert is served at more than 2 slots, and at least one expert at exactly 2. `routes_one`: the 2 entries of a token differ; in the rows of one device no expert is named more than 20 times, and in some device's rows one is named exactly 20 times. `routes_two`: the 2 entries of a token differ; in the rows of one device no slot is named more than 20 times, and in some device's rows one is named exactly 20 times.
All inputs are finite; a program needn't handle non-finite values.
Results may differ from a plain program's by a relative error of at most 0.006.
Values may be sent and summed in bfloat16 or wider, within the bound.
A program may use at most 128 MiB of HBM per device.

v0:
```python
import jax
import jax.numpy as jnp
from jax import lax
from jax.sharding import PartitionSpec as P

WIN_BLOCKS = 4
NBUCK = 32


score_scale = 0.125
epsilon = 1e-06
masked_score = -1e30


def prefix(x, axis, combine, identity):
    length, index = (lax.axis_size(axis), lax.axis_index(axis))
    everything = jax.tree.map(
        lambda part, kind: lax.all_gather(part.astype(kind), axis),
        x,
        jax.tree.map(lambda a: jnp.bfloat16 if a.dtype == jnp.float32 else a.dtype, x),
    )
    start = jax.tree.map(
        lambda part, zero: jnp.broadcast_to(jnp.asarray(zero, part.dtype), part.shape), x, identity
    )

    def lap(k, before):
        reached = k < index
        new = combine(
            before, jax.tree.map(lambda part, own: part[k].astype(own.dtype), everything, x)
        )
        return jax.tree.map(lambda a, b: jnp.where(reached, a, b), new, before)

    return lax.fori_loop(0, length, lap, start)


def passed_along(value, axis, steps):
    count = lax.axis_size(axis)
    initial, last = (max(0, -steps), min(count, count - steps))
    return lax.ppermute(value, axis, [(source, source + steps) for source in range(initial, last)])


def bit_length(distance):
    counted = jnp.zeros_like(distance)
    for exponent in range(NBUCK - 2):
        counted = counted + (distance >= 1 << exponent).astype(jnp.int32)
    return counted


def table_lookup(table, index, expert_ids):
    return jnp.sum(jnp.where(index[..., None] == expert_ids, table, 0), axis=-1)


def merge_starts(former, latter):
    take_latter = (latter[4] > 0) & ((former[4] == 0) | (latter[3] != former[3]))
    return tuple((jnp.where(take_latter, newer, older) for older, newer in zip(former, latter)))


def attend(queries, key_rows, value_rows, segments, bias_table, window_bias):
    tok_count = queries.shape[0]
    model_width = queries.shape[1]
    head_count = bias_table.shape[0]
    head_dim = model_width // head_count
    window_len = WIN_BLOCKS * tok_count
    block_start = lax.axis_index("seq") * tok_count
    positions = block_start + jnp.arange(tok_count, dtype=jnp.int32)
    last_seg = segments[tok_count - 1]
    lead_index = jnp.sum((segments < last_seg).astype(jnp.int32))
    candidate = (
        key_rows[lead_index],
        value_rows[lead_index],
        block_start + lead_index,
        last_seg,
        jnp.ones((), jnp.int32),
    )
    identity = (
        jnp.zeros((model_width,), key_rows.dtype),
        jnp.zeros((model_width,), value_rows.dtype),
        jnp.zeros((), jnp.int32),
        jnp.zeros((), jnp.int32),
        jnp.zeros((), jnp.int32),
    )
    sink_key, sink_value, sink_pos, sink_seg, sink_has = prefix(
        candidate, "seq", merge_starts, identity
    )
    local_first = jnp.sum((segments[None, :] < segments[:, None]).astype(jnp.int32), axis=1)
    from_before = (sink_has > 0) & (segments == sink_seg)
    starts = jnp.where(from_before, sink_pos, block_start + local_first)
    stacked = jnp.stack([key_rows, value_rows])
    fetched = []
    moving = stacked
    for hop_index in range(WIN_BLOCKS):
        moving = passed_along(moving, "seq", 1)
        fetched.append(moving)
    window_slab = jnp.concatenate(fetched[::-1] + [stacked], axis=1)
    key_slab = window_slab[0].reshape(window_len + tok_count, head_count, head_dim)
    value_slab = window_slab[1].reshape(window_len + tok_count, head_count, head_dim)
    query_heads = queries.reshape(tok_count, head_count, head_dim)
    scores = (
        jnp.einsum("qhd,khd->hqk", query_heads, key_slab, preferred_element_type=jnp.float32)
        * score_scale
        + window_bias
    )
    key_pos = block_start - window_len + jnp.arange(window_len + tok_count, dtype=jnp.int32)
    distance = positions[:, None] - key_pos[None, :]
    visible = (key_pos[None, :] >= starts[:, None]) & (distance >= 0) & (distance < window_len)
    scores = jnp.where(visible[None], scores, masked_score)
    sink_scores = (
        jnp.einsum(
            "qhd,hd->hq",
            query_heads,
            sink_key.reshape(head_count, head_dim),
            preferred_element_type=jnp.float32,
        )
        * score_scale
        + bias_table[:, NBUCK - 1][:, None]
    )
    sink_visible = positions - starts >= window_len
    sink_scores = jnp.where(sink_visible[None], sink_scores, masked_score)
    row_peak = jnp.maximum(jnp.max(scores, axis=2), sink_scores)
    weights = jnp.exp(scores - row_peak[:, :, None])
    sink_weight = jnp.exp(sink_scores - row_peak)
    row_total = jnp.sum(weights, axis=2) + sink_weight
    attn_probs = (weights / row_total[:, :, None]).astype(jnp.bfloat16)
    sink_prob = (sink_weight / row_total).astype(jnp.bfloat16)
    context = jnp.einsum("hqk,khd->qhd", attn_probs, value_slab, preferred_element_type=jnp.float32)
    context = context + jnp.einsum(
        "hq,hd->qhd",
        sink_prob,
        sink_value.reshape(head_count, head_dim),
        preferred_element_type=jnp.float32,
    )
    return context.reshape(tok_count, model_width).astype(jnp.bfloat16)


def expert_layer(normed, logits, chosen, target_dev, capacity, experts, matrices):
    gate_mat, up_mat, down_mat = matrices
    tok_count = normed.shape[0]
    model_width = normed.shape[1]
    top_count = chosen.shape[1]
    expert_ids = jnp.arange(experts, dtype=jnp.int32)
    picked = jnp.sum(jnp.where(chosen[:, :, None] == expert_ids, logits[:, None, :], 0.0), axis=2)
    first_gate = jax.nn.sigmoid(picked[:, 0] - picked[:, 1])
    gate_pair = jnp.stack([first_gate, 1.0 - first_gate], axis=1)
    flat_target = target_dev.reshape(-1)
    member = (flat_target[:, None] == expert_ids[None, :]).astype(jnp.int32)
    before = jnp.cumsum(member, axis=0) - member
    slot_index = jnp.sum(before * member, axis=1)
    placement = flat_target * capacity + slot_index
    send_plan = (
        placement[None, :] == jnp.arange(experts * capacity, dtype=jnp.int32)[:, None]
    ).astype(jnp.bfloat16)
    plan_tokens = jnp.sum(send_plan.reshape(experts * capacity, tok_count, top_count), axis=2)
    outgoing = (
        jnp.dot(plan_tokens, normed, preferred_element_type=jnp.float32)
        .astype(jnp.bfloat16)
        .reshape(experts, capacity, model_width)
    )
    received = lax.all_to_all(outgoing, "exp", split_axis=0, concat_axis=0, tiled=True)
    sources, item_count, inner_width = received.shape
    flat_rows = received.reshape(sources * item_count, inner_width)
    gate_part = jnp.dot(flat_rows, gate_mat, preferred_element_type=jnp.float32)
    up_part = jnp.dot(flat_rows, up_mat, preferred_element_type=jnp.float32)
    active = (jax.nn.gelu(gate_part, approximate=True) * up_part).astype(jnp.bfloat16)
    expert_out = jnp.dot(active, down_mat, preferred_element_type=jnp.float32).astype(jnp.bfloat16)
    answered = expert_out.reshape(sources, item_count, inner_width)
    returned = lax.all_to_all(answered, "exp", split_axis=0, concat_axis=0, tiled=True)
    pair_values = jnp.dot(
        send_plan.T,
        returned.reshape(experts * capacity, model_width),
        preferred_element_type=jnp.float32,
    )
    return jnp.sum(
        pair_values.reshape(tok_count, top_count, model_width) * gate_pair[:, :, None], axis=1
    )


def local(
    tokens,
    queries,
    key_rows,
    value_rows,
    segments,
    bias_table,
    out_proj,
    router,
    gate_weight,
    up_weight,
    down_weight,
    old_table,
    new_table,
    routes_one,
    routes_two,
):
    tok_count = tokens.shape[2]
    experts = router.shape[1]
    top_count = routes_one.shape[2]
    capacity = tok_count * top_count * 5 // (4 * experts)
    window_len = WIN_BLOCKS * tok_count
    dist_grid = (
        jnp.arange(tok_count, dtype=jnp.int32)[:, None]
        + window_len
        - jnp.arange(window_len + tok_count, dtype=jnp.int32)[None, :]
    )
    buckets = bit_length(jnp.maximum(dist_grid, 0))
    onehot = (buckets[:, :, None] == jnp.arange(NBUCK, dtype=jnp.int32)[None, None, :]).astype(
        jnp.float32
    )
    window_bias = jnp.einsum("qkn,hn->hqk", onehot, bias_table, precision=lax.Precision.HIGHEST)
    expert_ids = jnp.arange(experts, dtype=jnp.int32)
    holder_of = jnp.sum(
        jnp.where(old_table[:, None] == expert_ids[None, :], expert_ids[:, None], 0), axis=0
    )
    first_chosen = routes_one[0]
    first_target = table_lookup(holder_of, first_chosen, expert_ids)
    second_chosen = table_lookup(new_table, routes_two[0], expert_ids)
    own_mats = (gate_weight[0], up_weight[0], down_weight[0])
    seq_parts = lax.axis_size("seq")
    piece_width = gate_weight.shape[2] // seq_parts
    offset = lax.axis_index("seq") * piece_width
    needed = jnp.sum(jnp.where(expert_ids == lax.axis_index("exp"), new_table, 0))
    source_dev = jnp.sum(jnp.where(expert_ids == needed, holder_of, 0))
    pieces = (
        lax.dynamic_slice_in_dim(gate_weight, offset, piece_width, 2),
        lax.dynamic_slice_in_dim(up_weight, offset, piece_width, 2),
        lax.dynamic_slice_in_dim(down_weight, offset, piece_width, 1),
    )
    shard_piece = (
        lax.all_gather(pieces[0], "exp", axis=0, tiled=True),
        lax.all_gather(pieces[1], "exp", axis=0, tiled=True),
        lax.all_gather(pieces[2], "exp", axis=0, tiled=True),
    )
    rows_here = jnp.arange(shard_piece[0].shape[0], dtype=jnp.int32)
    wanted = rows_here == source_dev
    held_slices = tuple(
        (
            jnp.sum(
                jnp.where(wanted[:, None, None], part_piece, jnp.zeros_like(part_piece)), axis=0
            )
            for part_piece in shard_piece
        )
    )
    second_mats = (
        lax.all_gather(held_slices[0], "seq", axis=1, tiled=True),
        lax.all_gather(held_slices[1], "seq", axis=1, tiled=True),
        lax.all_gather(held_slices[2], "seq", axis=0, tiled=True),
    )
    second_target = routes_two[0]
    batch_plans = (
        (first_chosen, first_target, capacity, own_mats),
        (second_chosen, second_target, capacity, second_mats),
    )
    results = []
    for batch_index in range(2):
        context = attend(
            queries[batch_index, 0],
            key_rows[batch_index, 0],
            value_rows[batch_index, 0],
            segments[batch_index, 0],
            bias_table,
            window_bias,
        )
        hidden = tokens[batch_index, 0].astype(jnp.float32) + jnp.dot(
            context, out_proj, preferred_element_type=jnp.float32
        )
        normed = (
            hidden * lax.rsqrt(jnp.mean(hidden * hidden, axis=1, keepdims=True) + epsilon)
        ).astype(jnp.bfloat16)
        logits = jnp.dot(normed, router, preferred_element_type=jnp.float32)
        chosen, target_dev, slot_room, matrices = batch_plans[batch_index]
        mixed_out = expert_layer(normed, logits, chosen, target_dev, slot_room, experts, matrices)
        results.append((hidden + mixed_out).astype(jnp.bfloat16))
    return jnp.stack(results)[:, None]


def solution(mesh):
    placed = (
        P(None, "exp", "seq", None),
        P(None, "exp", "seq", None),
        P(None, "exp", "seq", None),
        P(None, "exp", "seq", None),
        P(None, "exp", "seq"),
        P(),
        P(),
        P(),
        P("exp", None, None),
        P("exp", None, None),
        P("exp", None, None),
        P(),
        P(),
        P("exp", "seq", None),
        P("exp", "seq", None),
    )
    return jax.shard_map(
        local, mesh=mesh, in_specs=placed, out_specs=P(None, "exp", "seq", None), check_vma=False
    )
```

profile of v0, /device:TPU:1, one launch (start us, length us, event | category | flops | bytes accessed | tf_op | source)
XLA Modules:
  0.0 616.4 jit_solution(10699190262741866518)
XLA Ops:
  11.5 2.3 fusion.118
  15.3 4.5 collective-permute-start
  25.0 2.0 fusion.103
  35.1 18.9 %all-gather.2 = bf16[16,1,1,1024]{3,2,1,0:T(2,128)(2,1)S(1)} all-gather(bf16[1,1,1,1024]{3,2,1,0:T(2,128)(2,1)S(1)} %constant_dynamic-slice_fusion.5), channel_id=4, replica_groups=mesh['seq'=16,'exp'=16] {'seq'}, dimensions={0}, use_global_device_ids=true | all-gather | bytes 34816 | tf_op jit(solution)/shard_map/all_gather | solution.py:18
  54.8 18.1 %all-gather.1 = bf16[16,1,1,1024]{3,2,1,0:T(2,128)(2,1)S(1)} all-gather(bf16[1,1,1,1024]{3,2,1,0:T(2,128)(2,1)S(1)} %constant_dynamic-slice_fusion.6), channel_id=3, replica_groups=mesh['seq'=16,'exp'=16] {'seq'}, dimensions={0}, use_global_device_ids=true | all-gather | bytes 34816 | tf_op jit(solution)/shard_map/all_gather | solution.py:18
  75.0 18.9 %all-gather.5 = bf16[16,1,1,1024]{3,2,1,0:T(2,128)(2,1)S(1)} all-gather(bf16[1,1,1,1024]{3,2,1,0:T(2,128)(2,1)S(1)} %constant_dynamic-slice_fusion.3), channel_id=7, replica_groups=mesh['seq'=16,'exp'=16] {'seq'}, dimensions={0}, use_global_device_ids=true | all-gather | bytes 34816 | tf_op jit(solution)/shard_map/all_gather | solution.py:18
  94.6 17.0 %all-gather.4 = bf16[16,1,1,1024]{3,2,1,0:T(2,128)(2,1)S(1)} all-gather(bf16[1,1,1,1024]{3,2,1,0:T(2,128)(2,1)S(1)} %constant_dynamic-slice_fusion.4), channel_id=6, replica_groups=mesh['seq'=16,'exp'=16] {'seq'}, dimensions={0}, use_global_device_ids=true | all-gather | bytes 34816 | tf_op jit(solution)/shard_map/all_gather | solution.py:18
  116.9 2.1 dynamic-update-slice.4
  119.7 9.4 %all-reduce.5 = (s32[16]{0:T(128)}, s32[16]{0:T(128)}, s32[16]{0:T(128)}, s32[16]{0:T(128)}, s32[16]{0:T(128)}) all-reduce(s32[16]{0:T(128)S(1)} %dynamic-update-slice, s32[16]{0:T(128)} %copy-done.44, s32[16]{0:T(128)} %copy-done.45, s32[16]{0:T(128)} %copy-done.43, s32[16]{0:T(128)} %dynamic-update-slice.4), channel_id=1, replica_groups=mesh['seq'=16,'exp'=16] {'seq'}, use_global_device_ids=true, to_apply=%add | all-reduce | flops 80 | bytes 640
  129.1 152.3 %while.44 = (s32[]{:T(128)}, bf16[1024]{0:T(1024)(128)(2,1)}, bf16[1024]{0:T(1024)(128)(2,1)}, s32[]{:T(128)}, s32[]{:T(128)}, /*index=5*/s32[]{:T(128)}, s32[]{...) while((s32[]{:T(128)}, bf16[1024]{0:T(1024)(128)(2,1)}, ...), condition=%wide.region_2.3_spmd.clone, body=%wide.region_1.2_spmd.clone.sunk | while | flops 6159 | bytes 20788 | solution.py:33
  281.6 4.8 select_reduce_fusion.2
  286.5 86.6 %while.45 = (s32[]{:T(128)}, bf16[1024]{0:T(1024)(128)(2,1)S(1)}, bf16[1024]{0:T(1024)(128)(2,1)S(1)}, s32[]{:T(128)}, s32[]{:T(128)}, /*index=5*/s32[]{:T(128)}...) while((s32[]{:T(128)}, bf16[1024]{0:T(1024)(128)(2,1)S(1)}, ...), condition=%wide.region_17.18_spmd.clone, body=%wide.region_16.17_spmd.clone.sunk | while | flops 6159 | bytes 20788 | solution.py:33
  381.3 5.9 fusion
  387.2 6.2 %copy.104 = f32[128,640,16]{0,1,2:T(8,128)} copy(f32[128,640,16]{1,2,0:T(8,128)} %fusion) | data formatting | bytes 10485760 | tf_op jit(solution)/shard_map/qkn,hn->hqk/dot_general | solution.py:208
  398.4 3.6 collective-permute-start.1
  403.0 2.1 collective-permute-start.5
  405.0 3.4 collective-permute-done.1
  408.5 4.4 collective-permute-start.2
  414.5 3.9 collective-permute-start.6
  420.1 4.3 collective-permute-start.3
  426.8 7.2 %collective-permute-done.6 = bf16[2,128,1024]{2,1,0:T(8,128)(2,1)} collective-permute-done((bf16[2,128,1024]{2,1,0:T(8,128)(2,1)S(1)}, bf16[2,128,1024]{2,1,0:T(8,128)(2,1)}, u32[]{:S(2)}, u32[]{:S(2)}) %collective-permute-start.6) | collective-permute-done | bytes 524320 | tf_op jit(solution)/shard_map/ppermute | solution.py:39
  434.0 4.6 collective-permute-start.7
  438.6 5.8 collective-permute-done.3
  448.4 2.4 copy.101
  456.9 2.5 copy.111
  459.4 2.4 copy.100
  461.9 4.4 fusion.121
  471.1 3.0 select_reduce_fusion
  474.3 4.2 fusion.40
  482.7 11.0 %all-to-all-start = ((bf16[16,20,1024]{2,1,0:T(8,128)(2,1)}), bf16[16,20,1024]{2,1,0:T(8,128)(2,1)}, u32[]{:S(2)}, u32[]{:S(2)}) async-start(bf16[16,20,1024]{2,1,0:T(8,128)(2,1)} %reshape.495), calls=%async_computation | async-start | bytes 1572864 | tf_op jit(solution)/shard_map/all_to_all | solution.py:158
  493.7 2.4 copy.110
  496.2 4.2 fusion.41
  505.0 20.4 %all-to-all-done = bf16[16,20,1024]{2,1,0:T(8,128)(2,1)} async-done(((bf16[16,20,1024]{2,1,0:T(8,128)(2,1)}), bf16[16,20,1024]{2,1,0:T(8,128)(2,1)}, u32[]{:S(2)}, u32[]{:S(2)}) %all-to-all-start) | async-done | bytes 655392 | tf_op jit(solution)/shard_map/all_to_all | solution.py:158
  525.4 4.5 all-to-all-start.2
  530.0 2.0 reshape.496
  532.0 3.6 fusion.23
  535.7 6.5 %fusion.33 = bf16[320,1024]{1,0:T(8,128)(2,1)} fusion(bf16[1,1408,1024]{2,1,0:T(8,128)(2,1)} %param.29, f32[320,1408]{1,0:T(8,128)} %fusion.23, bf16[320,1024]{1,0:T(8,128)(2,1)} %reshape.496, bf16[1,1024,1408]{2,1,0:T(8,128)(2,1)} %param.28), kind=kOutput, calls=%fused_computation.55 | convolution fusion | flops 1846722560 | bytes 8880128 | tf_op jit(solution)/shard_map/dot_general | solution.py:164
  542.1 2.0 reshape.497
  544.2 8.0 %all-to-all-done.2 = bf16[16,20,1024]{2,1,0:T(8,128)(2,1)} async-done(((bf16[16,20,1024]{2,1,0:T(8,128)(2,1)}), bf16[16,20,1024]{2,1,0:T(8,128)(2,1)}, u32[]{:S(2)}, u32[]{:S(2)}) %all-to-all-start.2) | async-done | bytes 655392 | tf_op jit(solution)/shard_map/all_to_all | solution.py:158
  552.2 4.3 all-to-all-start.1
  556.8 2.0 reshape.503
  558.8 4.5 fusion.125
  563.3 6.5 %convolution_convert_fusion.2 = bf16[320,1024]{1,0:T(8,128)(2,1)} fusion(bf16[1408,1024]{1,0:T(8,128)(2,1)} %all-gather.23.cloned.1.call-done, bf16[320,1024]{1,0:T(8,128)(2,1)} %reshape.503, bf16[1024,1408]{0,1:T(8,128)(2,1)} %all-gather.19.cloned.1.call-done, f32[320,1408]{1,0:T(8,128)} %fusion.125), kind=kOutput, calls=%fused_computation.56 | convolution fusion | flops 1850327040 | bytes 8880128 | tf_op jit(solution)/shard_map/dot_general | solution.py:164
  569.9 2.0 reshape.504
  571.9 7.7 %all-to-all-done.1 = bf16[16,20,1024]{2,1,0:T(8,128)(2,1)} async-done(((bf16[16,20,1024]{2,1,0:T(8,128)(2,1)}), bf16[16,20,1024]{2,1,0:T(8,128)(2,1)}, u32[]{:S(2)}, u32[]{:S(2)}) %all-to-all-start.1) | async-done | bytes 655392 | tf_op jit(solution)/shard_map/all_to_all | solution.py:166
  579.6 4.3 all-to-all-start.3
  585.2 2.0 reshape.546
  589.7 15.3 %all-to-all-done.3 = bf16[16,20,1024]{2,1,0:T(8,128)(2,1)} async-done(((bf16[16,20,1024]{2,1,0:T(8,128)(2,1)}), bf16[16,20,1024]{2,1,0:T(8,128)(2,1)}, u32[]{:S(2)}, u32[]{:S(2)}) %all-to-all-start.3) | async-done | bytes 655392 | tf_op jit(solution)/shard_map/all_to_all | solution.py:166
  (441 shorter events, 209.9 us)
Async XLA Ops:
  6.5 275.0 %all-gather.13.cloned.1.call-start = ((), (), s32[]{:S(2)}) async-start(), calls=%async_computation.4 | async-start | bytes 3063808 | tf_op jit(solution)/shard_map/all_gather | solution.py:228
  9.3 272.2 %all-gather.17.cloned.1.call-start = ((), (), s32[]{:S(2)}) async-start(), calls=%async_computation.6 | async-start | bytes 3063808 | tf_op jit(solution)/shard_map/all_gather | solution.py:229
  11.4 12.9 %copy-start.25 = (s32[2,1,128]{2,1,0:T(1,128)S(1)}, s32[2,1,128]{2,1,0:T(1,128)}, u32[]{:S(2)}) copy-start(s32[2,1,128]{2,1,0:T(1,128)} %param.23) | copy-start | bytes 3076
  11.4 18.2 %copy-start.49 = (u32[256]{0:T(256)S(1)}, u32[256]{0:T(256)}, u32[]{:S(2)}) copy-start(u32[256]{0:T(256)} %constant.183) | copy-start | bytes 3076
  11.4 100.9 %copy-start.39 = (s32[16]{0:T(128)S(1)}, s32[16]{0:T(128)}, u32[]{:S(2)}) copy-start(s32[16]{0:T(128)} %param.31) | copy-start | bytes 196
  11.4 459.7 %all-gather.21.cloned.1.call-start = ((), (), s32[]{:S(2)}) async-start(), calls=%async_computation.8 | async-start | bytes 3063808 | tf_op jit(solution)/shard_map/all_gather | solution.py:230
  15.3 383.1 %collective-permute-start = (bf16[2,128,1024]{2,1,0:T(8,128)(2,1)}, bf16[2,128,1024]{2,1,0:T(8,128)(2,1)}, u32[]{:S(2)}, u32[]{:S(2)}) collective-permute-start(bf16[2,128,1024]{2,1,0:T(8,128)(2,1)} %pad_maximum_fusion), channel_id=1, source_target_pairs={{0,16},{16,32},{32,48},{48,64},{64,80},{80,96},{96,112},{112,128},... | collective-permute-start | bytes 1572872 | tf_op jit(solution)/shard_map/ppermute | solution.py:39
  20.7 382.3 %collective-permute-start.4 = (bf16[2,128,1024]{2,1,0:T(8,128)(2,1)}, bf16[2,128,1024]{2,1,0:T(8,128)(2,1)}, u32[]{:S(2)}, u32[]{:S(2)}) collective-permute-start(bf16[2,128,1024]{2,1,0:T(8,128)(2,1)} %pad_maximum_fusion.1), channel_id=1, source_target_pairs={{0,16},{16,32},{32,48},{48,64},{64,80},{80,96},{96,112},{112,128},... | collective-permute-start | bytes 1572872 | tf_op jit(solution)/shard_map/ppermute | solution.py:39
  24.2 534.6 %all-gather.15.cloned.1.call-start = ((), (), s32[]{:S(2)}) async-start(), calls=%async_computation.5 | async-start | bytes 3063808 | tf_op jit(solution)/shard_map/all_gather | solution.py:243
  33.1 41.9 %copy-start.44 = (s32[16]{0:T(128)}, s32[16]{0:T(128)S(1)}, u32[]{:S(2)}) copy-start(s32[16]{0:T(128)S(1)} %bitcast_dynamic-update-slice_fusion.1) | copy-start | bytes 196
  112.3 16.8 %copy-start.41 = (s32[16]{0:T(128)}, s32[16]{0:T(128)S(1)}, u32[]{:S(2)}) copy-start(s32[16]{0:T(128)S(1)} %select_reduce_fusion.7) | copy-start | bytes 196
  281.4 5.0 copy-start.46
  281.4 5.0 copy-start.47
  281.5 5.0 copy-start.48
  281.5 91.7 %copy-start.32 = (s32[1,128,2]{1,2,0:T(2,128)S(1)}, s32[1,128,2]{1,2,0:T(2,128)}, u32[]{:S(2)}) copy-start(s32[1,128,2]{1,2,0:T(2,128)} %param.32) | copy-start | bytes 3076
  281.5 91.7 %copy-start.42 = (s32[16]{0:T(128)S(1)}, s32[16]{0:T(128)}, u32[]{:S(2)}) copy-start(s32[16]{0:T(128)} %copy-done.41) | copy-start | bytes 196
  281.5 92.2 %copy-start.27 = (s32[1,128,2]{1,2,0:T(2,128)S(1)}, s32[1,128,2]{1,2,0:T(2,128)}, u32[]{:S(2)}) copy-start(s32[1,128,2]{1,2,0:T(2,128)} %param.33) | copy-start | bytes 3076
  286.4 94.9 %copy-start.24 = (f32[16,32]{1,0:T(8,128)S(1)}, f32[16,32]{1,0:T(8,128)}, u32[]{:S(2)}) copy-start(f32[16,32]{1,0:T(8,128)} %param.24) | copy-start | bytes 6148
  286.4 276.9 %all-gather.19.cloned.1.call-start = ((), (), s32[]{:S(2)}) async-start(), calls=%async_computation.7 | async-start | bytes 3063808 | tf_op jit(solution)/shard_map/all_gather | solution.py:244
  387.2 8.0 %copy-start.22 = (bf16[1024]{0:T(1024)(128)(2,1)S(1)}, bf16[1024]{0:T(1024)(128)(2,1)}, u32[]{:S(2)}) copy-start(bf16[1024]{0:T(1024)(128)(2,1)} %get-tuple-element.414) | copy-start | bytes 6148
  387.2 8.2 %copy-start.23 = (bf16[1024]{0:T(1024)(128)(2,1)S(1)}, bf16[1024]{0:T(1024)(128)(2,1)}, u32[]{:S(2)}) copy-start(bf16[1024]{0:T(1024)(128)(2,1)} %get-tuple-element.415) | copy-start | bytes 6148
  387.2 11.3 %copy-start.26 = (s32[2,1,128]{2,1,0:T(1,128)S(1)}, s32[2,1,128]{2,1,0:T(1,128)}, u32[]{:S(2)}) copy-start(s32[2,1,128]{2,1,0:T(1,128)} %param.23) | copy-start | bytes 3076
  397.7 15.1 %copy-start.34 = (s32[128,2]{0,1:T(2,128)}, s32[128,2]{0,1:T(2,128)S(1)}, u32[]{:S(2)}) copy-start(s32[128,2]{0,1:T(2,128)S(1)} %multiply_add_fusion.1) | copy-start | bytes 3076
  398.4 10.0 %collective-permute-start.1 = (bf16[2,128,1024]{2,1,0:T(8,128)(2,1)}, bf16[2,128,1024]{2,1,0:T(8,128)(2,1)}, u32[]{:S(2)}, u32[]{:S(2)}) collective-permute-start(bf16[2,128,1024]{2,1,0:T(8,128)(2,1)} %collective-permute-done), channel_id=1, source_target_pairs={{0,16},{16,32},{32,48},{48,64},{64,80},{80,96},{96,112},{112,128},... | collective-permute-start | bytes 1572872 | tf_op jit(solution)/shard_map/ppermute | solution.py:39
  402.8 21.7 %copy-start.36 = (s32[128,2]{0,1:T(2,128)}, s32[128,2]{0,1:T(2,128)S(1)}, u32[]{:S(2)}) copy-start(s32[128,2]{0,1:T(2,128)S(1)} %multiply_add_fusion) | copy-start | bytes 3076
  402.9 160.4 %all-gather.23.cloned.1.call-start = ((), (), s32[]{:S(2)}) async-start(), calls=%async_computation.9 | async-start | bytes 3063808 | tf_op jit(solution)/shard_map/all_gather | solution.py:245
  402.9 43.7 %copy-start.9 = (bf16[1,128,1024]{2,1,0:T(8,128)(2,1)S(1)}, bf16[1,128,1024]{2,1,0:T(8,128)(2,1)}, u32[]{:S(2)}) copy-start(bf16[1,128,1024]{2,1,0:T(8,128)(2,1)} %copy-done.8) | copy-start | bytes 786436
  402.9 43.7 %copy-start.11 = (bf16[1,128,1024]{2,1,0:T(8,128)(2,1)S(1)}, bf16[1,128,1024]{2,1,0:T(8,128)(2,1)}, u32[]{:S(2)}) copy-start(bf16[1,128,1024]{2,1,0:T(8,128)(2,1)} %copy-done.10) | copy-start | bytes 786436
  403.0 11.5 %collective-permute-start.5 = (bf16[2,128,1024]{2,1,0:T(8,128)(2,1)}, bf16[2,128,1024]{2,1,0:T(8,128)(2,1)S(1)}, u32[]{:S(2)}, u32[]{:S(2)}) collective-permute-start(bf16[2,128,1024]{2,1,0:T(8,128)(2,1)} %collective-permute-done.4), channel_id=1, source_target_pairs={{0,16},{16,32},{32,48},{48,64},{64,80},{80,96},{96,112},{112,128},... | collective-permute-start | bytes 1572872 | tf_op jit(solution)/shard_map/ppermute | solution.py:39
  408.5 11.6 %collective-permute-start.2 = (bf16[2,128,1024]{2,1,0:T(8,128)(2,1)}, bf16[2,128,1024]{2,1,0:T(8,128)(2,1)S(1)}, u32[]{:S(2)}, u32[]{:S(2)}) collective-permute-start(bf16[2,128,1024]{2,1,0:T(8,128)(2,1)} %collective-permute-done.1), channel_id=1, source_target_pairs={{0,16},{16,32},{32,48},{48,64},{64,80},{80,96},{96,112},{112,128},... | collective-permute-start | bytes 1572872 | tf_op jit(solution)/shard_map/ppermute | solution.py:39
  413.6 54.5 %copy-start.28 = (pred[128]{0:T(512)(128)(4,1)}, pred[128]{0:T(512)(128)(4,1)S(1)}, u32[]{:S(2)}) copy-start(pred[128]{0:T(512)(128)(4,1)S(1)} %get-tuple-element.558) | copy-start | bytes 388
  413.6 54.5 %copy-start.30 = (pred[128]{0:T(512)(128)(4,1)}, pred[128]{0:T(512)(128)(4,1)S(1)}, u32[]{:S(2)}) copy-start(pred[128]{0:T(512)(128)(4,1)S(1)} %get-tuple-element.588) | copy-start | bytes 388
  414.5 24.1 %copy-start.15 = (bf16[2,128,1024]{2,1,0:T(8,128)(2,1)}, bf16[2,128,1024]{2,1,0:T(8,128)(2,1)S(1)}, u32[]{:S(2)}) copy-start(bf16[2,128,1024]{2,1,0:T(8,128)(2,1)S(1)} %collective-permute-done.5) | copy-start | bytes 1572868
  414.5 19.5 %collective-permute-start.6 = (bf16[2,128,1024]{2,1,0:T(8,128)(2,1)S(1)}, bf16[2,128,1024]{2,1,0:T(8,128)(2,1)}, u32[]{:S(2)}, u32[]{:S(2)}) collective-permute-start(bf16[2,128,1024]{2,1,0:T(8,128)(2,1)S(1)} %collective-permute-done.5), channel_id=1, source_target_pairs={{0,16},{16,32},{32,48},{48,64},{64,80},{80,96},{96,112},{112,128},... | collective-permute-start | bytes 1572872 | tf_op jit(solution)/shard_map/ppermute | solution.py:39
  420.1 24.3 %collective-permute-start.3 = (bf16[2,128,1024]{2,1,0:T(8,128)(2,1)S(1)}, bf16[2,128,1024]{2,1,0:T(8,128)(2,1)S(1)}, u32[]{:S(2)}, u32[]{:S(2)}) collective-permute-start(bf16[2,128,1024]{2,1,0:T(8,128)(2,1)S(1)} %collective-permute-done.2), channel_id=1, source_target_pairs={{0,16},{16,32},{32,48},{48,64},{64,80},{80,96},{96,112},{112,128},... | collective-permute-start | bytes 1572872 | tf_op jit(solution)/shard_map/ppermute | solution.py:39
  434.0 16.9 %collective-permute-start.7 = (bf16[2,128,1024]{2,1,0:T(8,128)(2,1)}, bf16[2,128,1024]{2,1,0:T(8,128)(2,1)}, u32[]{:S(2)}, u32[]{:S(2)}) collective-permute-start(bf16[2,128,1024]{2,1,0:T(8,128)(2,1)} %collective-permute-done.6), channel_id=1, source_target_pairs={{0,16},{16,32},{32,48},{48,64},{64,80},{80,96},{96,112},{112,128},... | collective-permute-start | bytes 1572872 | tf_op jit(solution)/shard_map/ppermute | solution.py:39
  456.9 4.9 copy-start.13
  456.9 4.9 copy-start.20
  482.7 42.7 %all-to-all-start = ((bf16[16,20,1024]{2,1,0:T(8,128)(2,1)}), bf16[16,20,1024]{2,1,0:T(8,128)(2,1)}, u32[]{:S(2)}, u32[]{:S(2)}) async-start(bf16[16,20,1024]{2,1,0:T(8,128)(2,1)} %reshape.495), calls=%async_computation | async-start | bytes 1572864 | tf_op jit(solution)/shard_map/all_to_all | solution.py:158
  501.0 28.9 %copy-start.40 = (s32[16]{0:T(128)S(1)}, s32[16]{0:T(128)}, u32[]{:S(2)}) copy-start(s32[16]{0:T(128)} %param.31) | copy-start | bytes 196
  525.4 26.8 %all-to-all-start.2 = ((bf16[16,20,1024]{2,1,0:T(8,128)(2,1)}), bf16[16,20,1024]{2,1,0:T(8,128)(2,1)}, u32[]{:S(2)}, u32[]{:S(2)}) async-start(bf16[16,20,1024]{2,1,0:T(8,128)(2,1)} %reshape.502), calls=%async_computation.2 | async-start | bytes 1572864 | tf_op jit(solution)/shard_map/all_to_all | solution.py:158
  542.1 14.4 %copy-start.21 = (bf16[1024,16]{0,1:T(8,128)(2,1)S(1)}, bf16[1024,16]{0,1:T(8,128)(2,1)}, u32[]{:S(2)}) copy-start(bf16[1024,16]{0,1:T(8,128)(2,1)} %param.26) | copy-start | bytes 98308
  542.1 14.6 %copy-start.33 = (s32[1,128,2]{1,2,0:T(2,128)S(1)}, s32[1,128,2]{1,2,0:T(2,128)}, u32[]{:S(2)}) copy-start(s32[1,128,2]{1,2,0:T(2,128)} %param.32) | copy-start | bytes 3076
  552.2 27.3 %all-to-all-start.1 = ((bf16[16,20,1024]{2,1,0:T(8,128)(2,1)}), bf16[16,20,1024]{2,1,0:T(8,128)(2,1)}, u32[]{:S(2)}, u32[]{:S(2)}) async-start(bf16[16,20,1024]{2,1,0:T(8,128)(2,1)} %reshape.497), calls=%async_computation.1 | async-start | bytes 1572864 | tf_op jit(solution)/shard_map/all_to_all | solution.py:166
  569.9 17.4 %copy-start.35 = (s32[128,2]{0,1:T(2,128)S(1)}, s32[128,2]{0,1:T(2,128)}, u32[]{:S(2)}) copy-start(s32[128,2]{0,1:T(2,128)} %copy-done.34) | copy-start | bytes 3076
  579.6 25.4 %all-to-all-start.3 = ((bf16[16,20,1024]{2,1,0:T(8,128)(2,1)}), bf16[16,20,1024]{2,1,0:T(8,128)(2,1)}, u32[]{:S(2)}, u32[]{:S(2)}) async-start(bf16[16,20,1024]{2,1,0:T(8,128)(2,1)} %reshape.504), calls=%async_computation.3 | async-start | bytes 1572864 | tf_op jit(solution)/shard_map/all_to_all | solution.py:166
  585.2 21.7 %copy-start.37 = (s32[128,2]{0,1:T(2,128)S(1)}, s32[128,2]{0,1:T(2,128)}, u32[]{:S(2)}) copy-start(s32[128,2]{0,1:T(2,128)} %copy-done.36) | copy-start | bytes 3076
  589.7 18.9 %copy-start.6 = (f32[128,1024]{1,0:T(8,128)S(1)}, f32[128,1024]{1,0:T(8,128)}, u32[]{:S(2)}) copy-start(f32[128,1024]{1,0:T(8,128)} %copy-done.5) | copy-start | bytes 1572868
  (22 other events, 64.4 us)
Sparse Core Ops, SparseCore 0:
  9.8 69.1 all-gather.12
  81.5 63.9 all-gather.16
  148.0 63.7 all-gather.20
  286.5 42.2 all-gather.14
  403.0 43.8 all-gather.18
  474.3 54.6 all-gather.22
where the time goes:
time: 621 us; the launch traced here: 616 us
  local copies, waits for them, and re-layouts  169 us (27%)
  loops' own time  105 us (17%)
  blocking collectives  82.2 us (13%)
  waiting for transfers between devices  69.6 us (11%)
  other arithmetic  65.2 us (10%)
  starting transfers between devices  53.5 us (9%)
  matrix products  51.8 us (8%)
  between operations  19.6 us (3%)
    another operation x2, loops' own time, prefix(): return lax.fori_loop(0, length, lap, start)  105 us
    dynamic_slice x128, local copies, waits for them, and re-layouts, lap(): part[k].astype(own.dtype)  93.8 us
    all_gather x4, blocking collectives, prefix(): lax.all_gather(part.astype(kind), axis)  72.8 us
    select_n x64, other arithmetic, lap(): return jax.tree.map(lambda a, b: jnp.where(reached, a, b), new, before)  39.7 us
    ppermute x8, starting transfers between devices, passed_along(): lax.ppermute(value, axis, [(source, source + steps) for source in range(i...  29.2 us
    all_to_all x2, waiting for transfers between devices, expert_layer(): lax.all_to_all(outgoing, 'exp', split_axis=0, concat_axis=0, tiled=True)  28.4 us
    all_to_all x2, waiting for transfers between devices, expert_layer(): lax.all_to_all(answered, 'exp', split_axis=0, concat_axis=0, tiled=True)  23 us
    unnamed x130, local copies, waits for them, and re-layouts  21.6 us
  transfers between devices with their start and end apart: 18, of which 8 were waited for; matrix products, arithmetic and copies ran while one was open for 45% of the time, Pallas kernels for 0%

commit v1 on v0

v1 whole, which is shorter than its diff:
```python
import jax
import jax.numpy as jnp
from jax import lax
from jax.experimental import pallas as pl
from jax.experimental.pallas import tpu as pltpu
from jax.sharding import PartitionSpec as P

MESH = pl.DeviceIdType.MESH
BF16 = jnp.bfloat16
F32 = jnp.float32
I32 = jnp.int32

N_SEQ = 16
N_EXP = 16
EXP_Y = 4
EXP_Z = 4
TOK = 128
D = 1024
FFW = 1408
NBUCK = 32
WIN = 4
PAIRS = 8
LANES = 128
HALF = 64
CAP = 20
ROWS = 64
FIRST_ROWS = 24
SINK_BUCKET = 31

EPSILON = 1e-06
MASKED = -1e30


def iota(shape, dim):
    return lax.broadcasted_iota(I32, shape, dim)


def dot(a, b):
    return jnp.dot(a, b, preferred_element_type=F32)


def dot_t(a, b):
    return lax.dot_general(a, b, (((1,), (1,)), ((), ())), preferred_element_type=F32)


def greet(axis, count):
    me = lax.axis_index(axis)
    barrier = pltpu.get_barrier_semaphore()
    for step in range(1, count):
        pl.semaphore_signal(
            barrier, inc=1, device_id={axis: lax.rem(me + step, count)}, device_id_type=MESH
        )
    pl.semaphore_wait(barrier, count - 1)


def bias_of_distance(distance, values):
    result = jnp.full(distance.shape, values[0], F32)
    for bucket in range(1, 10):
        result = jnp.where(distance >= (1 << (bucket - 1)), values[bucket], result)
    return result


def attention_kernel(
    table,
    q_hbm,
    k_hbm,
    v_hbm,
    seg_hbm,
    out_hbm,
    qb,
    kb,
    vb,
    segs,
    segcol,
    bias,
    sink_rows,
    ctx,
    send_sem,
    recv_sem,
    local_sem,
    out_send,
    out_recv,
    out_local,
):
    me = lax.axis_index("seq")
    greet("seq", N_SEQ)

    def parts(target, spot):
        batch = target // PAIRS
        lanes = pl.ds(pl.multiple_of(lax.rem(target, PAIRS) * LANES, LANES), LANES)
        return (
            (k_hbm.at[batch, 0, :, lanes], kb.at[spot + WIN]),
            (v_hbm.at[batch, 0, :, lanes], vb.at[spot + WIN]),
            (q_hbm.at[batch, 0, :, lanes], qb.at[spot]),
            (seg_hbm.at[batch], segs.at[spot + WIN]),
        )

    copies = []
    for step in range(1, N_SEQ):
        target = lax.rem(me + step, N_SEQ)
        for kind, (src, dst) in enumerate(parts(target, me)):
            copy = pltpu.make_async_remote_copy(
                src_ref=src,
                dst_ref=dst,
                send_sem=send_sem.at[kind, step],
                recv_sem=recv_sem.at[kind, step],
                device_id={"seq": target},
                device_id_type=MESH,
            )
            copy.start()
            copies.append(copy)
    own = []
    for kind, (src, dst) in enumerate(parts(me, me)):
        copy = pltpu.make_async_copy(src, dst, local_sem.at[kind])
        copy.start()
        own.append(copy)

    kb[0:WIN] = jnp.zeros((WIN, TOK, LANES), BF16)
    vb[0:WIN] = jnp.zeros((WIN, TOK, LANES), BF16)
    segs[0:WIN] = jnp.full((WIN, 1, TOK), -1, I32)
    first_head = 2 * lax.rem(me, PAIRS)
    qi = iota((TOK, TOK), 0)
    kj = iota((TOK, TOK), 1)
    for head in range(2):
        values = [table[first_head + head, bucket] for bucket in range(10)]
        rows = slice(head * TOK, (head + 1) * TOK)
        merged = jnp.where(kj <= qi, qi - kj, qi - kj + WIN * TOK)
        bias[0, rows, :] = bias_of_distance(merged, values)
        for block in range(1, WIN):
            bias[block, rows, :] = bias_of_distance(qi - kj + (WIN - block) * TOK, values)
    sink_bias = jnp.where(
        iota((2 * TOK, 1), 0) < TOK,
        table[first_head, SINK_BUCKET],
        table[first_head + 1, SINK_BUCKET],
    )

    for copy in own:
        copy.wait()
    for copy in copies:
        copy.wait()

    def columns(block, before):
        row = segs[block]
        segcol[block] = jnp.transpose(jnp.broadcast_to(row, (TOK, TOK)))
        document = iota((8, TOK), 0)
        return before + jnp.where((row < document) & (row >= 0), 1, 0)

    ahead = lax.fori_loop(0, N_SEQ + WIN, columns, jnp.zeros((8, TOK), I32))
    starts = jnp.sum(ahead, axis=1, keepdims=True)

    def sinks(block, sums):
        k_sum, v_sum = sums
        spot = block * TOK + iota((8, TOK), 1)
        pick = jnp.where(spot == starts, 1.0, 0.0).astype(BF16)
        return (k_sum + dot(pick, kb[block + WIN]), v_sum + dot(pick, vb[block + WIN]))

    zero = jnp.zeros((8, LANES), F32)
    k_sink, v_sink = lax.fori_loop(0, N_SEQ, sinks, (zero, zero))
    sink_rows[0] = k_sink
    sink_rows[1] = v_sink

    lane_head = iota((2 * TOK, LANES), 1) // HALF
    row_head = iota((2 * TOK, LANES), 0) // TOK
    own_half = lane_head == row_head
    causal = lax.rem(iota((2 * TOK, TOK), 0), TOK) >= iota((2 * TOK, TOK), 1)

    def twice(value):
        return jnp.concatenate([value, value], axis=0)

    def attend(block, carry):
        query = twice(qb[block].astype(F32) * 0.125)
        query = jnp.where(own_half, query, 0.0)
        query_rows = query.astype(BF16)
        mine = segcol[block + WIN]
        pieces = []
        for near in range(WIN + 1):
            raw = dot_t(query_rows, kb[block + near])
            same = twice(mine == segs[block + near])
            pieces.append((raw, same))
        merged = jnp.where(causal, pieces[WIN][0], pieces[0][0])
        merged_same = jnp.where(
            causal, pieces[WIN][1].astype(I32), pieces[0][1].astype(I32)
        )
        scores = [jnp.where(merged_same > 0, merged + bias[0], MASKED)]
        for near in range(1, WIN):
            raw, same = pieces[near]
            scores.append(jnp.where(same, raw + bias[near], MASKED))
        chosen_doc = iota((8, LANES), 0) == segs[block + WIN][:, 0:1]
        k_row = jnp.sum(jnp.where(chosen_doc, sink_rows[0], 0.0), axis=0, keepdims=True)
        v_row = jnp.sum(jnp.where(chosen_doc, sink_rows[1], 0.0), axis=0, keepdims=True)
        sink_seen = twice(mine[:, 0:1] == segcol[block][:, 0:1])
        sink = jnp.sum(query * k_row, axis=1, keepdims=True) + sink_bias
        sink = jnp.where(sink_seen, sink, MASKED)
        peak = jnp.maximum(jnp.maximum(scores[0], scores[1]), jnp.maximum(scores[2], scores[3]))
        peak = jnp.maximum(jnp.max(peak, axis=1, keepdims=True), sink)
        weights = [jnp.exp(score - peak) for score in scores]
        sink_weight = jnp.exp(sink - peak)
        total = (weights[0] + weights[1]) + (weights[2] + weights[3])
        total = jnp.sum(total, axis=1, keepdims=True) + sink_weight
        mixed = sink_weight * v_row
        mixed = mixed + dot(jnp.where(causal, 0.0, weights[0]).astype(BF16), vb[block])
        mixed = mixed + dot(jnp.where(causal, weights[0], 0.0).astype(BF16), vb[block + WIN])
        for near in range(1, WIN):
            mixed = mixed + dot(weights[near].astype(BF16), vb[block + near])
        mixed = mixed / total
        ctx[block] = jnp.where(
            lane_head[:TOK] == 0, mixed[:TOK], mixed[TOK:]
        ).astype(BF16)
        return carry

    lax.fori_loop(0, N_SEQ, attend, 0)

    batch = me // PAIRS
    lanes = pl.ds(pl.multiple_of(lax.rem(me, PAIRS) * LANES, LANES), LANES)
    outgoing = []
    for step in range(1, N_SEQ):
        target = lax.rem(me + step, N_SEQ)
        copy = pltpu.make_async_remote_copy(
            src_ref=ctx.at[target],
            dst_ref=out_hbm.at[batch, :, lanes],
            send_sem=out_send.at[step],
            recv_sem=out_recv.at[step],
            device_id={"seq": target},
            device_id_type=MESH,
        )
        copy.start()
        outgoing.append(copy)
    mine = pltpu.make_async_copy(ctx.at[me], out_hbm.at[batch, :, lanes], out_local)
    mine.start()
    mine.wait()
    for copy in outgoing:
        copy.wait()


def attention(bias_table, queries, key_rows, value_rows, segments):
    any_spec = pl.BlockSpec(memory_space=pl.ANY)
    return pl.pallas_call(
        attention_kernel,
        out_shape=jax.ShapeDtypeStruct((2, TOK, D), BF16),
        in_specs=[pl.BlockSpec(memory_space=pltpu.SMEM)] + [any_spec] * 4,
        out_specs=any_spec,
        scratch_shapes=[
            pltpu.VMEM((N_SEQ, TOK, LANES), BF16),
            pltpu.VMEM((N_SEQ + WIN, TOK, LANES), BF16),
            pltpu.VMEM((N_SEQ + WIN, TOK, LANES), BF16),
            pltpu.VMEM((N_SEQ + WIN, 1, TOK), I32),
            pltpu.VMEM((N_SEQ + WIN, TOK, TOK), I32),
            pltpu.VMEM((WIN, 2 * TOK, TOK), F32),
            pltpu.VMEM((2, 8, LANES), F32),
            pltpu.VMEM((N_SEQ, TOK, LANES), BF16),
            pltpu.SemaphoreType.DMA((4, N_SEQ)),
            pltpu.SemaphoreType.DMA((4, N_SEQ)),
            pltpu.SemaphoreType.DMA((4,)),
            pltpu.SemaphoreType.DMA((N_SEQ,)),
            pltpu.SemaphoreType.DMA((N_SEQ,)),
            pltpu.SemaphoreType.DMA(()),
        ],
        compiler_params=pltpu.CompilerParams(
            collective_id=0, has_side_effects=True, vmem_limit_bytes=32 << 20
        ),
        name="attention",
    )(bias_table, queries, key_rows, value_rows, segments)


def plane_step(group):
    return group + (group // 2) * (1 - 2 * lax.rem(group, 2))


def expert_kernel(
    ctx,
    tokens,
    out_proj,
    router,
    routes_one,
    routes_two,
    bases,
    serving,
    gate_hbm,
    up_hbm,
    down_hbm,
    out_ref,
    gate_w,
    up_w,
    down_w,
    hidden,
    normed,
    sbuf,
    rbuf,
    ybuf,
    back,
    active,
    w_sem,
    send_sem,
    recv_sem,
    back_send,
    back_recv,
):
    me = lax.axis_index("exp")
    me_y, me_z = me // EXP_Z, lax.rem(me, EXP_Z)
    loads = [
        pltpu.make_async_copy(gate_hbm.at[0], gate_w, w_sem.at[0]),
        pltpu.make_async_copy(up_hbm.at[0], up_w, w_sem.at[1]),
        pltpu.make_async_copy(down_hbm.at[0], down_w, w_sem.at[2]),
    ]
    for load in loads:
        load.start()

    context = ctx[...].reshape(2 * TOK, D)
    for part in range(2):
        cols = slice(part * 512, (part + 1) * 512)
        hidden[:, cols] = tokens[:, 0, :, cols].reshape(2 * TOK, 512).astype(F32) + dot(
            context, out_proj[:, cols]
        )
    rows_value = hidden[...]
    scale = lax.rsqrt(jnp.mean(rows_value * rows_value, axis=1, keepdims=True) + EPSILON)
    normed[...] = (rows_value * scale).astype(BF16)
    logits = dot(normed[...], router[...])

    lane = iota((TOK, LANES), 1)
    lower = jnp.where(iota((TOK, TOK), 0) > lane, 1.0, 0.0).astype(BF16)
    places, weights = [], []
    for batch, routes in enumerate((routes_one, routes_two)):
        named = [routes[0, :, c : c + 1] == lane for c in range(2)]
        member = [jnp.where(hit, 1.0, 0.0) for hit in named]
        member_b = [m.astype(BF16) for m in member]
        counts = [dot(lower, m) for m in member_b]
        counts[1] = counts[1] + jnp.sum(member[0], axis=0, keepdims=True)
        base = bases[batch : batch + 1, :]
        places.append(
            [
                jnp.sum(m * (c + base), axis=1, keepdims=True)
                for m, c in zip(member, counts)
            ]
        )
        difference = member[0] - member[1]
        if batch == 1:
            difference = dot(difference.astype(BF16), serving[...])
        picked = jnp.sum(
            difference[:, :N_EXP] * logits[batch * TOK : (batch + 1) * TOK], axis=1, keepdims=True
        )
        first = jax.nn.sigmoid(picked)
        weights.append([first, 1.0 - first])
    place_rows = [
        jnp.concatenate(
            [
                jnp.transpose(jnp.broadcast_to(places[batch][c], (TOK, TOK)))[0:1, :]
                for batch in range(2)
            ],
            axis=1,
        )
        for c in range(2)
    ]

    greet("exp", N_EXP)

    def target_of(group, dy, sign):
        y = lax.rem(me_y + EXP_Y + sign * dy, EXP_Y)
        z = lax.rem(me_z + EXP_Z + sign * plane_step(group), EXP_Z)
        return y * EXP_Z + z

    outgoing = []
    for group in (3, 1, 2, 0):
        spot = (iota((EXP_Y * ROWS, 2 * TOK), 0) + group * EXP_Y * ROWS).astype(F32)
        plan = jnp.where((spot == place_rows[0]) | (spot == place_rows[1]), 1.0, 0.0).astype(BF16)
        for part in range(2):
            cols = slice(part * 512, (part + 1) * 512)
            sbuf[group * EXP_Y : (group + 1) * EXP_Y, :, cols] = (
                dot(plan, normed[:, cols]).astype(BF16).reshape(EXP_Y, ROWS, 512)
            )
        for dy in range(EXP_Y):
            slot = group * EXP_Y + dy
            if slot == 0:
                continue
            copy = pltpu.make_async_remote_copy(
                src_ref=sbuf.at[slot],
                dst_ref=rbuf.at[slot],
                send_sem=send_sem.at[slot],
                recv_sem=recv_sem.at[slot],
                device_id={"exp": target_of(group, dy, 1)},
                device_id_type=MESH,
            )
            copy.start()
            outgoing.append(copy)
    rbuf[0] = sbuf[0]
    for load in loads:
        load.wait()

    def answer(slot, group, dy):
        return pltpu.make_async_remote_copy(
            src_ref=ybuf.at[slot],
            dst_ref=back.at[slot],
            send_sem=back_send.at[slot],
            recv_sem=back_recv.at[slot],
            device_id={"exp": target_of(group, dy, -1)},
            device_id_type=MESH,
        )

    def arrival(slot, group, dy):
        return pltpu.make_async_remote_copy(
            src_ref=sbuf.at[slot],
            dst_ref=rbuf.at[slot],
            send_sem=send_sem.at[slot],
            recv_sem=recv_sem.at[slot],
            device_id={"exp": target_of(group, dy, 1)},
            device_id_type=MESH,
        )

    def serve(group, carry):
        for dy in range(EXP_Y):
            slot = group * EXP_Y + dy
            if dy == 0:

                @pl.when(group > 0)
                def _():
                    arrival(slot, group, dy).wait_recv()

            else:
                arrival(slot, group, dy).wait_recv()
        inputs = rbuf[pl.ds(group * EXP_Y, EXP_Y)].reshape(EXP_Y * ROWS, D)
        for low, high in ((0, 512), (512, 1024), (1024, FFW)):
            gate = dot(inputs, gate_w[:, low:high])
            up = dot(inputs, up_w[:, low:high])
            inner = 0.7978845608028654 * (gate + 0.044715 * (gate * gate * gate))
            active[:, low:high] = (0.5 * gate * (1.0 + jnp.tanh(inner)) * up).astype(BF16)
        for part in range(2):
            cols = slice(part * 512, (part + 1) * 512)
            ybuf[pl.ds(group * EXP_Y, EXP_Y), :, cols] = (
                dot(active[...], down_w[:, cols]).astype(BF16).reshape(EXP_Y, ROWS, 512)
            )
        for dy in range(EXP_Y):
            slot = group * EXP_Y + dy
            if dy == 0:

                @pl.when(group > 0)
                def _():
                    answer(slot, group, dy).start()

            else:
                answer(slot, group, dy).start()
        return carry

    lax.fori_loop(0, EXP_Z, serve, 0)
    back[0] = ybuf[0]

    result = hidden[...]
    for group in range(EXP_Z):
        for dy in range(EXP_Y):
            if group + dy > 0:
                answer(group * EXP_Y + dy, group, dy).wait_recv()
        spot = (iota((TOK, EXP_Y * ROWS), 1) + group * EXP_Y * ROWS).astype(F32)
        mixes = []
        for batch in range(2):
            mixes.append(
                jnp.where(spot == places[batch][0], weights[batch][0], 0.0)
                + jnp.where(spot == places[batch][1], weights[batch][1], 0.0)
            )
        mix = jnp.concatenate(mixes, axis=0)
        coarse = mix.astype(BF16)
        fine = (mix - coarse.astype(F32)).astype(BF16)
        rows = back[group * EXP_Y : (group + 1) * EXP_Y].reshape(EXP_Y * ROWS, D)
        result = result + dot(coarse, rows) + dot(fine, rows)
    out_ref[...] = result.astype(BF16).reshape(2, 1, TOK, D)
    for copy in outgoing:
        copy.wait_send()
    for group in range(EXP_Z):
        for dy in range(EXP_Y):
            if group + dy > 0:
                answer(group * EXP_Y + dy, group, dy).wait_send()


def experts(
    ctx, tokens, out_proj, router, routes_one, routes_two, bases, serving, gate_w, up_w, down_w
):
    vmem = pl.BlockSpec(memory_space=pltpu.VMEM)
    any_spec = pl.BlockSpec(memory_space=pl.ANY)
    buffer = pltpu.VMEM((N_EXP, ROWS, D), BF16)
    sems = pltpu.SemaphoreType.DMA((N_EXP,))
    return pl.pallas_call(
        expert_kernel,
        out_shape=jax.ShapeDtypeStruct((2, 1, TOK, D), BF16),
        in_specs=[vmem] * 8 + [any_spec] * 3,
        out_specs=vmem,
        scratch_shapes=[
            pltpu.VMEM((D, FFW), BF16),
            pltpu.VMEM((D, FFW), BF16),
            pltpu.VMEM((FFW, D), BF16),
            pltpu.VMEM((2 * TOK, D), F32),
            pltpu.VMEM((2 * TOK, D), BF16),
            buffer,
            buffer,
            buffer,
            buffer,
            pltpu.VMEM((EXP_Y * ROWS, FFW), BF16),
            pltpu.SemaphoreType.DMA((3,)),
            sems,
            sems,
            sems,
            sems,
        ],
        compiler_params=pltpu.CompilerParams(
            collective_id=1, has_side_effects=True, vmem_limit_bytes=56 << 20
        ),
        name="experts",
    )(ctx, tokens, out_proj, router, routes_one, routes_two, bases, serving, gate_w, up_w, down_w)


def slot_tables(old_table, new_table):
    ids = jnp.arange(N_EXP, dtype=I32)
    me = lax.axis_index("exp")
    steps_y = lax.rem(ids // EXP_Z - me // EXP_Z + EXP_Y, EXP_Y)
    steps_z = lax.rem(lax.rem(ids, EXP_Z) - lax.rem(me, EXP_Z) + EXP_Z, EXP_Z)
    start_of = (plane_step(steps_z) * EXP_Y + steps_y) * ROWS
    held = old_table[:, None] == ids[None, :]
    first = jnp.sum(jnp.where(held, start_of[:, None], 0), axis=0)
    serving = new_table[:, None] == ids[None, :]
    second = jnp.sum(jnp.where(serving, first[None, :], 0), axis=1)
    repeated = (new_table[:, None] == new_table[None, :]) & (ids[None, :] < ids[:, None])
    second = second + FIRST_ROWS + CAP * jnp.sum(repeated.astype(I32), axis=1)
    bases = jnp.stack([first, second]).astype(F32)
    bases = jnp.pad(bases, ((0, 6), (0, LANES - N_EXP)))
    table = jnp.pad(serving.astype(BF16), ((0, LANES - N_EXP), (0, LANES - N_EXP)))
    return bases, table


def local(
    tokens,
    queries,
    key_rows,
    value_rows,
    segments,
    bias_table,
    out_proj,
    router,
    gate_weight,
    up_weight,
    down_weight,
    old_table,
    new_table,
    routes_one,
    routes_two,
):
    bases, serving = slot_tables(old_table, new_table)
    ctx = attention(bias_table, queries, key_rows, value_rows, segments)
    return experts(
        ctx,
        tokens,
        out_proj,
        router,
        routes_one,
        routes_two,
        bases,
        serving,
        gate_weight,
        up_weight,
        down_weight,
    )


def solution(mesh):
    placed = (
        P(None, "exp", "seq", None),
        P(None, "exp", "seq", None),
        P(None, "exp", "seq", None),
        P(None, "exp", "seq", None),
        P(None, "exp", "seq"),
        P(),
        P(),
        P(),
        P("exp", None, None),
        P("exp", None, None),
        P("exp", None, None),
        P(),
        P(),
        P("exp", "seq", None),
        P("exp", "seq", None),
    )
    return jax.shard_map(
        local, mesh=mesh, in_specs=placed, out_specs=P(None, "exp", "seq", None), check_vma=False
    )
```

time: 621 us -> 187 us (0.30)
  Pallas kernels: 0 us -> 171 us
  local copies, waits for them, and re-layouts: 169 us -> 12.1 us
  loops' own time: 105 us -> 0 us
  blocking collectives: 82.2 us -> 0 us
  waiting for transfers between devices: 69.6 us -> 0 us
  other arithmetic: 65.2 us -> 3.03 us
  starting transfers between devices: 53.5 us -> 0 us
  matrix products: 51.8 us -> 0 us
  between operations: 19.6 us -> 0.04 us
    pallas_call x0 -> x2, Pallas kernels: none -> 171 us  [the longest x1 116 us: experts(): pl.pallas_call(expert_kernel, out_shape=jax.ShapeDtypeStruct((2, 1, TOK,...]
    another operation x2 -> x0, loops' own time: 105 us -> none  [prefix(): return lax.fori_loop(0, length, lap, start)]
    dynamic_slice x135 -> x0, local copies, waits for them, and re-layouts: 99.7 us -> none  [the longest x128 93.8 us: lap(): part[k].astype(own.dtype)]
    all_gather x4 -> x0, blocking collectives: 72.8 us -> none  [prefix(): lax.all_gather(part.astype(kind), axis)]
    dot_general x19 -> x0, matrix products: 51.8 us -> none  [the longest x2 13 us: expert_layer(): jnp.dot(active, down_mat, preferred_element_type=jnp.float32)]
    all_to_all x4 -> x0, waiting for transfers between devices: 51.4 us -> none  [the longest x2 28.4 us: expert_layer(): lax.all_to_all(outgoing, 'exp', split_axis=0, concat_axis=0, tiled=True)]
    select_n x64 -> x0, other arithmetic: 39.7 us -> none  [lap(): return jax.tree.map(lambda a, b: jnp.where(reached, a, b), new, before)]
    ppermute x8 -> x0, starting transfers between devices: 29.2 us -> none  [passed_along(): lax.ppermute(value, axis, [(source, source + steps) for source in range(i...]
  transfers between devices with their start and end apart: 18 -> 0, of which waited for: 8 -> 0; matrix products, arithmetic and copies ran while one was open for 45% -> 0% of each run, Pallas kernels for 0% -> 0%
where the time goes in v1:
time: 187 us; the launch traced here: 186 us
  Pallas kernels  171 us (91%)
  local copies, waits for them, and re-layouts  12.1 us (6%)
  other arithmetic  3.03 us (2%)
    pallas_call x1, Pallas kernels, experts(): pl.pallas_call(expert_kernel, out_shape=jax.ShapeDtypeStruct((2, 1, TOK,...  116 us
    pallas_call x1, Pallas kernels, attention(): pl.pallas_call(attention_kernel, out_shape=jax.ShapeDtypeStruct((2, TOK,...  54.9 us
    unnamed x16, local copies, waits for them, and re-layouts  11.6 us

profile of v1, /device:TPU:1, one launch (start us, length us, event | category | flops | bytes accessed | tf_op | source)
XLA Modules:
  0.0 186.0 jit_solution(14188536169452722561)
XLA Ops:
  0.0 0.7 select_reduce_fusion.1
  0.8 0.9 select_reduce_fusion
  1.7 0.7 iota_compare_fusion.1
  2.4 0.6 pad.10.bases
  3.0 0.6 pad_convert_fusion.serving
  3.6 1.4 copy.17.routes_one
  5.0 1.4 copy.18.routes_two
  6.4 1.6 copy.16.router
  8.0 0.0 copy-start.1
  8.0 1.0 copy-done.1
  9.1 0.0 copy-start.2
  9.1 1.0 copy-done.2
  10.1 0.0 copy-start.3
  10.1 1.0 copy-done.3
  11.2 0.0 copy-start.4
  11.2 0.7 copy-done.4
  11.9 0.0 copy-start.5
  11.9 0.7 copy-done.5
  12.5 54.9 %attention.1.ctx = bf16[2,128,1024]{2,1,0:T(8,128)(2,1)S(1)} custom-call(f32[16,32]{1,0:T(8,128)S(1)} %copy-done.4, bf16[2,1,128,1024]{3,2,1,0:T(8,128)(2,1)S(1)} %copy-done.1, bf16[2,1,128,1024]{3,2,1,0:T(8,128)(2,1)S(1)} %copy-done.2, bf16[2,1,128,1024]{3,2,1,0:T(8,128)(2,1)S(1)} %copy-done.3, s32[2,1,128]{2,1,0:T(1,128)S(1)} %copy-done.5), custom_call_target="tpu_custom_call" | custom-call | tf_op jit(solution)/shard_map/attention/pallas_call | solution.py:237
  67.4 0.0 copy-start
  67.5 0.8 copy-done
  68.2 115.9 %experts.1 = bf16[2,1,128,1024]{3,2,1,0:T(8,128)(2,1)} custom-call(bf16[2,128,1024]{2,1,0:T(8,128)(2,1)} %copy-done, bf16[2,1,128,1024]{3,2,1,0:T(8,128)(2,1)} %tokens.1, bf16[1024,1024]{1,0:T(8,128)(2,1)} %out_proj.1, bf16[1024,16]{1,0:T(8,128)(2,1)} %copy.16.router, s32[1,128,2]{2,1,0:T(8,128)} %copy.17.routes_one, s32[1,128,2]{2,1,0:T(8,128)} %copy.18.routes_two, ...), custom_call_target="tpu_custom_call" | custom-call | tf_op jit(solution)/shard_map/experts/pallas_call | solution.py:478
  184.2 1.9 %copy.20 = bf16[2,1,128,1024]{3,2,1,0:T(8,128)(2,1)} copy(bf16[2,1,128,1024]{3,2,1,0:T(8,128)(2,1)} %experts.1) | data formatting | bytes 1048576
  (3 shorter events, 0.0 us)
Async XLA Ops:
  8.0 1.0 copy-start.1
  9.1 1.0 copy-start.2
  10.1 1.0 copy-start.3
  11.2 0.7 copy-start.4
  11.9 0.7 copy-start.5
  67.4 0.8 copy-start

commit v2 on v0

v2 whole, which is shorter than its diff:
```python
import jax
import jax.numpy as jnp
from jax import lax
from jax.experimental import pallas as pl
from jax.experimental.pallas import tpu as pltpu
from jax.sharding import PartitionSpec as P

MESH = pl.DeviceIdType.MESH
BF16 = jnp.bfloat16
F32 = jnp.float32
I32 = jnp.int32

N_SEQ = 16
N_EXP = 16
EXP_Y = 4
EXP_Z = 4
TOK = 128
D = 1024
FFW = 1408
NBUCK = 32
WIN = 4
PAIRS = 8
LANES = 128
HALF = 64
CAP = 20
STRIDE = (32, 48)
SENT = (24, 40)
SINK_BUCKET = 31
ORDER = (1, 0)

EPSILON = 1e-06
MASKED = -1e30


def iota(shape, dim):
    return lax.broadcasted_iota(I32, shape, dim)


def dot(a, b):
    return jnp.dot(a, b, preferred_element_type=F32)


def dot_t(a, b):
    return lax.dot_general(a, b, (((1,), (1,)), ((), ())), preferred_element_type=F32)


def turned(row):
    return jnp.transpose(jnp.broadcast_to(row, (LANES, LANES)))


def remote(src, dst, send, recv, **device):
    return pltpu.make_async_remote_copy(
        src_ref=src,
        dst_ref=dst,
        send_sem=send,
        recv_sem=recv,
        device_id=device,
        device_id_type=MESH,
    )


def bias_of_distance(distance, values):
    result = jnp.broadcast_to(values[0], distance.shape)
    for bucket in range(1, 10):
        result = jnp.where(distance >= (1 << (bucket - 1)), values[bucket], result)
    return result


def plane_step(group):
    return group + (group // 2) * (1 - 2 * lax.rem(group, 2))


def layer_kernel(
    bias_hbm,
    seg_hbm,
    q_hbm,
    k_hbm,
    v_hbm,
    tok_hbm,
    proj_hbm,
    router_hbm,
    one_hbm,
    two_hbm,
    old_hbm,
    new_hbm,
    gate_hbm,
    up_hbm,
    down_hbm,
    out_ref,
    table,
    routes,
    held,
    tabs,
    router,
    tok,
    proj,
    gate_w,
    up_w,
    down_w,
    segs,
    qb,
    kb,
    vb,
    segcol,
    bias,
    sink_out,
    sink_in,
    sink_rows,
    ctx_out,
    ctx_in,
    hidden,
    normed,
    sbuf_one,
    sbuf_two,
    rbuf_one,
    rbuf_two,
    ybuf_one,
    ybuf_two,
    back_one,
    back_two,
    active,
    load_sem,
    qkv_send,
    qkv_recv,
    qkv_own,
    seg_send,
    seg_recv,
    seg_own,
    hop_send,
    hop_recv,
    sink_send,
    sink_recv,
    ctx_send,
    ctx_recv,
    ctx_own,
    go_send,
    go_recv,
    back_send,
    back_recv,
):
    me = lax.axis_index("seq")
    my_exp = lax.axis_index("exp")
    upper, pair = me // PAIRS, lax.rem(me, PAIRS)
    me_y, me_z = my_exp // EXP_Z, lax.rem(my_exp, EXP_Z)
    first_of_half = upper * PAIRS
    across = lax.rem(me + PAIRS, N_SEQ)
    sbuf, rbuf = (sbuf_one, sbuf_two), (rbuf_one, rbuf_two)
    ybuf, back = (ybuf_one, ybuf_two), (back_one, back_two)

    early = [
        pltpu.make_async_copy(src, dst, load_sem.at[i])
        for i, (src, dst) in enumerate(
            (
                (old_hbm, held.at[0]),
                (new_hbm, held.at[1]),
                (one_hbm.at[0], routes.at[0]),
                (two_hbm.at[0], routes.at[1]),
                (bias_hbm, table),
            )
        )
    ]
    late = [
        pltpu.make_async_copy(src, dst, load_sem.at[i + 5])
        for i, (src, dst) in enumerate(
            (
                (router_hbm, router),
                (tok_hbm, tok),
                (proj_hbm, proj),
                (gate_hbm.at[0], gate_w),
                (up_hbm.at[0], up_w),
                (down_hbm.at[0], down_w),
            )
        )
    ]
    for copy in early:
        copy.start()

    for batch in range(2):
        low = STRIDE[batch] - 16
        back[batch][:, low:, :] = jnp.zeros((N_EXP, 16, D), BF16)

    @pl.when(upper == 0)
    def _():
        for batch in range(2):
            kb[batch, 0:WIN] = jnp.zeros((WIN, TOK, LANES), BF16)
            vb[batch, 0:WIN] = jnp.zeros((WIN, TOK, LANES), BF16)
            segs[batch, 0:PAIRS] = jnp.full((PAIRS, 1, TOK), -1, I32)
            sink_in[batch] = jnp.zeros((2, 8, LANES), F32)

    barrier = pltpu.get_barrier_semaphore()
    for step in range(1, PAIRS):
        pl.semaphore_signal(
            barrier,
            inc=1,
            device_id={"seq": first_of_half + lax.rem(pair + step, PAIRS)},
            device_id_type=MESH,
        )
    pl.semaphore_signal(barrier, inc=1, device_id={"seq": across}, device_id_type=MESH)
    for step in range(1, N_EXP):
        pl.semaphore_signal(
            barrier,
            inc=1,
            device_id={"exp": lax.rem(my_exp + step, N_EXP)},
            device_id_type=MESH,
        )
    pl.semaphore_wait(barrier, PAIRS + N_EXP - 1)

    def lanes_of(which):
        return pl.ds(pl.multiple_of(which * LANES, LANES), LANES)

    def qkv_parts(batch, target):
        lanes = lanes_of(target)
        return (
            (k_hbm.at[batch, 0, :, lanes], kb.at[batch, pair + WIN]),
            (v_hbm.at[batch, 0, :, lanes], vb.at[batch, pair + WIN]),
            (q_hbm.at[batch, 0, :, lanes], qb.at[batch, pair]),
        )

    def qkv_copies(batch):
        copies = []
        for step in range(1, PAIRS):
            target = lax.rem(pair + step, PAIRS)
            for kind, (src, dst) in enumerate(qkv_parts(batch, target)):
                copies.append(
                    remote(
                        src,
                        dst,
                        qkv_send.at[batch, kind, step],
                        qkv_recv.at[batch, kind, step],
                        seq=first_of_half + target,
                    )
                )
        for kind, (src, dst) in enumerate(qkv_parts(batch, pair)):
            copies.append(pltpu.make_async_copy(src, dst, qkv_own.at[batch, kind]))
        return copies

    qkv = [qkv_copies(batch) for batch in range(2)]
    seg_copies = [
        remote(
            seg_hbm,
            segs.at[:, PAIRS + pair],
            seg_send.at[step],
            seg_recv.at[step],
            seq=first_of_half + lax.rem(pair + step, PAIRS),
        )
        for step in range(1, PAIRS)
    ]
    seg_copies.append(pltpu.make_async_copy(seg_hbm, segs.at[:, PAIRS + pair], seg_own))
    seg_hop = remote(
        segs.at[:, PAIRS : 2 * PAIRS],
        segs.at[:, 0:PAIRS],
        hop_send.at[4],
        hop_recv.at[4],
        seq=across,
    )

    def halo_hop(batch, kind):
        block = (kb, vb)[kind]
        return remote(
            block.at[batch, PAIRS : PAIRS + WIN],
            block.at[batch, 0:WIN],
            hop_send.at[2 * batch + kind],
            hop_recv.at[2 * batch + kind],
            seq=across,
        )

    def sink_hop(batch):
        return remote(
            sink_out.at[batch],
            sink_in.at[batch],
            sink_send.at[batch],
            sink_recv.at[batch],
            seq=across,
        )

    for copy in seg_copies:
        copy.start()
    for copy in qkv[ORDER[0]]:
        copy.start()
    for copy in late:
        copy.start()
    for copy in early:
        copy.wait()

    qi = iota((TOK, TOK), 0)
    kj = iota((TOK, TOK), 1)
    for head in range(2):
        head_row = table[pl.ds(2 * pair + head, 1), :]
        values = [head_row[:, bucket : bucket + 1] for bucket in range(10)]
        rows = slice(head * TOK, (head + 1) * TOK)
        merged = jnp.where(kj <= qi, qi - kj, qi - kj + WIN * TOK)
        bias[0, rows, :] = bias_of_distance(merged, values)
        for block in range(1, WIN):
            bias[block, rows, :] = bias_of_distance(qi - kj + (WIN - block) * TOK, values)
    sink_bias = jnp.where(
        iota((2 * TOK, 1), 0) < TOK,
        table[pl.ds(2 * pair, 1), :][:, SINK_BUCKET : SINK_BUCKET + 1],
        table[pl.ds(2 * pair + 1, 1), :][:, SINK_BUCKET : SINK_BUCKET + 1],
    )

    lane = iota((LANES, LANES), 1)
    row = iota((LANES, LANES), 0)
    tabs[...] = jnp.full((2, LANES), -1, I32)
    tabs[0:1, 0:N_EXP] = held[0]
    tabs[1:2, 0:N_EXP] = held[1]
    steps_y = lax.rem(row // EXP_Z - me_y + 2 * EXP_Y * EXP_Y, EXP_Y)
    steps_z = lax.rem(lax.rem(row, EXP_Z) - me_z + EXP_Z, EXP_Z)
    groups = steps_z + (steps_z // 2) * (1 - 2 * lax.rem(steps_z, 2))
    slot_of_row = (groups * EXP_Y + steps_y).astype(F32)
    holds = turned(tabs[0:1, :]) == lane
    slot_of_expert = jnp.sum(jnp.where(holds, slot_of_row, 0.0), axis=0, keepdims=True)
    new_row = tabs[1:2, :]
    new_col = turned(new_row)
    served = new_col == lane
    serving = jnp.where(served, 1.0, 0.0).astype(BF16)
    slot_two = jnp.sum(jnp.where(served, slot_of_expert, 0.0), axis=1, keepdims=True)
    again = jnp.where((new_col == new_row) & (lane < row), 1.0, 0.0)
    again = jnp.sum(again, axis=1, keepdims=True)
    base_two = jnp.transpose(
        jnp.broadcast_to(slot_two * STRIDE[1] + again * CAP, (LANES, LANES))
    )[0:1, :]
    bases = (slot_of_expert * STRIDE[0], base_two)
    lower = jnp.where(row > lane, 1.0, 0.0).astype(BF16)
    place_cols, place_rows, differences = [], [], []
    for batch in range(2):
        member = [
            jnp.where(turned(routes[batch, c : c + 1, :]) == lane, 1.0, 0.0) for c in range(2)
        ]
        counts = [dot(lower, m.astype(BF16)) for m in member]
        counts[1] = counts[1] + jnp.sum(member[0], axis=0, keepdims=True)
        cols = [
            jnp.sum(m * (c + bases[batch]), axis=1, keepdims=True)
            for m, c in zip(member, counts)
        ]
        place_cols.append(cols)
        place_rows.append(
            [jnp.transpose(jnp.broadcast_to(col, (TOK, TOK)))[0:1, :] for col in cols]
        )
        difference = member[0] - member[1]
        if batch == 1:
            difference = dot(difference.astype(BF16), serving)
        differences.append(difference)

    lane_head = iota((2 * TOK, LANES), 1) // HALF
    row_head = iota((2 * TOK, LANES), 0) // TOK
    own_half = lane_head == row_head
    causal = lax.rem(iota((2 * TOK, TOK), 0), TOK) >= iota((2 * TOK, TOK), 1)

    def twice(value):
        return jnp.concatenate([value, value], axis=0)

    def context_copy(batch, block):
        return remote(
            ctx_out.at[batch, block],
            ctx_in.at[batch, :, lanes_of(pair)],
            ctx_send.at[batch, block],
            ctx_recv.at[batch, pair],
            seq=first_of_half + block,
        )

    def context_own(batch):
        return pltpu.make_async_copy(
            ctx_out.at[batch, pair], ctx_in.at[batch, :, lanes_of(pair)], ctx_own.at[batch]
        )

    def attention(batch, opening):
        if opening:
            for copy in seg_copies:
                copy.wait()

            @pl.when(upper == 0)
            def _():
                seg_hop.start()

        for copy in qkv[batch]:
            copy.wait()

        @pl.when(upper == 0)
        def _():
            for kind in range(2):
                halo_hop(batch, kind).start()

        if opening:
            for copy in qkv[ORDER[1]]:
                copy.start()

            @pl.when(upper == 1)
            def _():
                seg_hop.wait_recv()

        def columns(block, before):
            line = segs[batch, block]
            segcol[block] = turned(line)
            document = iota((8, TOK), 0)
            return before + jnp.where((line < document) & (line >= 0), 1, 0)

        ahead = lax.fori_loop(0, 2 * PAIRS, columns, jnp.zeros((8, TOK), I32))
        starts = jnp.sum(ahead, axis=1, keepdims=True)

        def sinks(block, sums):
            k_sum, v_sum = sums
            spot = (upper * PAIRS + block) * TOK + iota((8, TOK), 1)
            pick = jnp.where(spot == starts, 1.0, 0.0).astype(BF16)
            return (
                k_sum + dot(pick, kb[batch, block + WIN]),
                v_sum + dot(pick, vb[batch, block + WIN]),
            )

        zero = jnp.zeros((8, LANES), F32)
        k_sink, v_sink = lax.fori_loop(0, PAIRS, sinks, (zero, zero))
        sink_out[batch, 0] = k_sink
        sink_out[batch, 1] = v_sink

        @pl.when(upper == 0)
        def _():
            sink_hop(batch).start()

        @pl.when(upper == 1)
        def _():
            sink_hop(batch).wait_recv()

        sink_rows[0] = k_sink + sink_in[batch, 0]
        sink_rows[1] = v_sink + sink_in[batch, 1]

        def attend(block):
            query = twice(qb[batch, block].astype(F32) * 0.125)
            query = jnp.where(own_half, query, 0.0)
            query_rows = query.astype(BF16)
            mine = segcol[block + PAIRS]
            pieces = []
            for near in range(WIN + 1):
                raw = dot_t(query_rows, kb[batch, block + near])
                same = twice(mine == segs[batch, block + near + WIN])
                pieces.append((raw, same))
            merged = jnp.where(causal, pieces[WIN][0], pieces[0][0])
            merged_same = jnp.where(
                causal, pieces[WIN][1].astype(I32), pieces[0][1].astype(I32)
            )
            scores = [jnp.where(merged_same > 0, merged + bias[0], MASKED)]
            for near in range(1, WIN):
                raw, same = pieces[near]
                scores.append(jnp.where(same, raw + bias[near], MASKED))
            chosen_doc = iota((8, LANES), 0) == segs[batch, block + PAIRS][:, 0:1]
            k_row = jnp.sum(jnp.where(chosen_doc, sink_rows[0], 0.0), axis=0, keepdims=True)
            v_row = jnp.sum(jnp.where(chosen_doc, sink_rows[1], 0.0), axis=0, keepdims=True)
            sink_seen = twice(mine[:, 0:1] == segcol[block + WIN][:, 0:1])
            sink = jnp.sum(query * k_row, axis=1, keepdims=True) + sink_bias
            sink = jnp.where(sink_seen, sink, MASKED)
            peak = jnp.maximum(
                jnp.maximum(scores[0], scores[1]), jnp.maximum(scores[2], scores[3])
            )
            peak = jnp.maximum(jnp.max(peak, axis=1, keepdims=True), sink)
            weights = [jnp.exp(score - peak) for score in scores]
            sink_weight = jnp.exp(sink - peak)
            total = (weights[0] + weights[1]) + (weights[2] + weights[3])
            total = jnp.sum(total, axis=1, keepdims=True) + sink_weight
            mixed = sink_weight * v_row
            mixed = mixed + dot(jnp.where(causal, 0.0, weights[0]).astype(BF16), vb[batch, block])
            mixed = mixed + dot(
                jnp.where(causal, weights[0], 0.0).astype(BF16), vb[batch, block + WIN]
            )
            for near in range(1, WIN):
                mixed = mixed + dot(weights[near].astype(BF16), vb[batch, block + near])
            mixed = mixed / total
            ctx_out[batch, block] = jnp.where(
                lane_head[:TOK] == 0, mixed[:TOK], mixed[TOK:]
            ).astype(BF16)

            @pl.when(block == pair)
            def _():
                context_own(batch).start()

            @pl.when(block != pair)
            def _():
                context_copy(batch, block).start()

        def attend_late(turn, carry):
            attend(WIN + lax.rem(pair + turn, WIN))
            return carry

        def attend_early(turn, carry):
            attend(lax.rem(pair + turn, WIN))
            return carry

        lax.fori_loop(0, WIN, attend_late, 0)

        @pl.when(upper == 1)
        def _():
            for kind in range(2):
                halo_hop(batch, kind).wait_recv()

        lax.fori_loop(0, WIN, attend_early, 0)

    def target_of(group, dy, sign):
        y = lax.rem(me_y + EXP_Y + sign * dy, EXP_Y)
        z = lax.rem(me_z + EXP_Z + sign * plane_step(group), EXP_Z)
        return y * EXP_Z + z

    def dispatch(batch, group, dy):
        slot = group * EXP_Y + dy
        rows = slice(0, SENT[batch])
        return remote(
            sbuf[batch].at[slot, rows],
            rbuf[batch].at[slot, rows],
            go_send.at[batch, slot],
            go_recv.at[batch, slot],
            exp=target_of(group, dy, 1),
        )

    def answer(batch, group, dy):
        slot = group * EXP_Y + dy
        rows = slice(0, SENT[batch])
        return remote(
            ybuf[batch].at[slot, rows],
            back[batch].at[slot, rows],
            back_send.at[batch, slot],
            back_recv.at[batch, slot],
            exp=target_of(group, dy, -1),
        )

    gates = [None, None]

    def front(batch, opening):
        for step in range(1, PAIRS):
            source = lax.rem(pair + step, PAIRS)
            remote(
                ctx_out.at[batch, source],
                ctx_in.at[batch, :, lanes_of(source)],
                ctx_send.at[batch, source],
                ctx_recv.at[batch, source],
                seq=first_of_half + source,
            ).wait_recv()
        context_own(batch).wait()
        if opening:
            for copy in late[:3]:
                copy.wait()
        context = ctx_in[batch]
        for part in range(2):
            cols = slice(part * 512, (part + 1) * 512)
            hidden[batch, :, cols] = tok[batch, 0, :, cols].astype(F32) + dot(
                context, proj[:, cols]
            )
        value = hidden[batch]
        scale = lax.rsqrt(jnp.mean(value * value, axis=1, keepdims=True) + EPSILON)
        normed[...] = (value * scale).astype(BF16)
        stride = STRIDE[batch]
        for group in (3, 1, 2, 0):
            spot = (iota((EXP_Y * stride, TOK), 0) + group * EXP_Y * stride).astype(F32)
            hit = (spot == place_rows[batch][0]) | (spot == place_rows[batch][1])
            plan = jnp.where(hit, 1.0, 0.0).astype(BF16)
            for part in range(2):
                cols = slice(part * 512, (part + 1) * 512)
                sbuf[batch][group * EXP_Y : (group + 1) * EXP_Y, :, cols] = (
                    dot(plan, normed[:, cols]).astype(BF16).reshape(EXP_Y, stride, 512)
                )
            for dy in range(EXP_Y):
                if group + dy > 0:
                    dispatch(batch, group, dy).start()
        rbuf[batch][0] = sbuf[batch][0]
        logits = dot_t(normed[...], router[...])
        picked = jnp.sum(differences[batch][:, :N_EXP] * logits, axis=1, keepdims=True)
        first = jax.nn.sigmoid(picked)
        gates[batch] = (first, 1.0 - first)

    def serve_all(batch):
        stride = STRIDE[batch]
        count = EXP_Y * stride

        def serve(group, carry):
            for dy in range(EXP_Y):
                if dy == 0:

                    @pl.when(group > 0)
                    def _():
                        dispatch(batch, group, dy).wait_recv()

                else:
                    dispatch(batch, group, dy).wait_recv()
            inputs = rbuf[batch][pl.ds(group * EXP_Y, EXP_Y)].reshape(count, D)
            for low, high in ((0, 512), (512, 1024), (1024, FFW)):
                gate = dot(inputs, gate_w[:, low:high])
                up = dot(inputs, up_w[:, low:high])
                inner = 0.7978845608028654 * (gate + 0.044715 * (gate * gate * gate))
                active[0:count, low:high] = (0.5 * gate * (1.0 + jnp.tanh(inner)) * up).astype(
                    BF16
                )
            for part in range(2):
                cols = slice(part * 512, (part + 1) * 512)
                ybuf[batch][pl.ds(group * EXP_Y, EXP_Y), :, cols] = (
                    dot(active[0:count], down_w[:, cols])
                    .astype(BF16)
                    .reshape(EXP_Y, stride, 512)
                )
            for dy in range(EXP_Y):
                if dy == 0:

                    @pl.when(group > 0)
                    def _():
                        answer(batch, group, dy).start()

                else:
                    answer(batch, group, dy).start()
            return carry

        lax.fori_loop(0, EXP_Z, serve, 0)
        back[batch][0] = ybuf[batch][0]

    def combine(batch):
        stride = STRIDE[batch]
        result = hidden[batch]
        for group in range(EXP_Z):
            for dy in range(EXP_Y):
                if group + dy > 0:
                    answer(batch, group, dy).wait_recv()
            spot = (iota((TOK, EXP_Y * stride), 1) + group * EXP_Y * stride).astype(F32)
            mix = jnp.where(spot == place_cols[batch][0], gates[batch][0], 0.0) + jnp.where(
                spot == place_cols[batch][1], gates[batch][1], 0.0
            )
            coarse = mix.astype(BF16)
            fine = (mix - coarse.astype(F32)).astype(BF16)
            rows = back[batch][group * EXP_Y : (group + 1) * EXP_Y].reshape(EXP_Y * stride, D)
            both = dot(jnp.concatenate([coarse, fine], axis=0), rows)
            result = result + both[:TOK] + both[TOK:]
        out_ref[batch, 0] = result.astype(BF16)

    for turn, batch in enumerate(ORDER):
        attention(batch, turn == 0)
        front(batch, turn == 0)
    for copy in late[3:]:
        copy.wait()
    for batch in ORDER:
        serve_all(batch)
    for batch in ORDER:
        combine(batch)

    for batch in range(2):
        for group in range(EXP_Z):
            for dy in range(EXP_Y):
                if group + dy > 0:
                    dispatch(batch, group, dy).wait_send()
                    answer(batch, group, dy).wait_send()
        for step in range(1, PAIRS):
            context_copy(batch, lax.rem(pair + step, PAIRS)).wait_send()

    @pl.when(upper == 0)
    def _():
        seg_hop.wait_send()
        for batch in range(2):
            sink_hop(batch).wait_send()
            for kind in range(2):
                halo_hop(batch, kind).wait_send()


def local(
    tokens,
    queries,
    key_rows,
    value_rows,
    segments,
    bias_table,
    out_proj,
    router,
    gate_weight,
    up_weight,
    down_weight,
    old_table,
    new_table,
    routes_one,
    routes_two,
):
    any_spec = pl.BlockSpec(memory_space=pl.ANY)
    vmem = pltpu.VMEM
    dma = pltpu.SemaphoreType.DMA
    buffers = [vmem((N_EXP, stride, D), BF16) for stride in STRIDE]
    return pl.pallas_call(
        layer_kernel,
        out_shape=jax.ShapeDtypeStruct((2, 1, TOK, D), BF16),
        in_specs=[any_spec] * 15,
        out_specs=pl.BlockSpec(memory_space=pltpu.VMEM),
        scratch_shapes=[
            vmem((N_EXP, NBUCK), F32),
            vmem((2, 2, TOK), I32),
            vmem((2, 1, N_EXP), I32),
            vmem((2, LANES), I32),
            vmem((N_EXP, D), BF16),
            vmem((2, 1, TOK, D), BF16),
            vmem((D, D), BF16),
            vmem((D, FFW), BF16),
            vmem((D, FFW), BF16),
            vmem((FFW, D), BF16),
            vmem((2, N_SEQ, 1, TOK), I32),
            vmem((2, PAIRS, TOK, LANES), BF16),
            vmem((2, PAIRS + WIN, TOK, LANES), BF16),
            vmem((2, PAIRS + WIN, TOK, LANES), BF16),
            vmem((N_SEQ, TOK, TOK), I32),
            vmem((WIN, 2 * TOK, TOK), F32),
            vmem((2, 2, 8, LANES), F32),
            vmem((2, 2, 8, LANES), F32),
            vmem((2, 8, LANES), F32),
            vmem((2, PAIRS, TOK, LANES), BF16),
            vmem((2, TOK, D), BF16),
            vmem((2, TOK, D), F32),
            vmem((TOK, D), BF16),
            *buffers,
            *buffers,
            *buffers,
            *buffers,
            vmem((EXP_Y * STRIDE[1], FFW), BF16),
            dma((11,)),
            dma((2, 3, PAIRS)),
            dma((2, 3, PAIRS)),
            dma((2, 3)),
            dma((PAIRS,)),
            dma((PAIRS,)),
            dma(()),
            dma((5,)),
            dma((5,)),
            dma((2,)),
            dma((2,)),
            dma((2, PAIRS)),
            dma((2, PAIRS)),
            dma((2,)),
            dma((2, N_EXP)),
            dma((2, N_EXP)),
            dma((2, N_EXP)),
            dma((2, N_EXP)),
        ],
        compiler_params=pltpu.CompilerParams(
            collective_id=0, has_side_effects=True, vmem_limit_bytes=56 << 20
        ),
        name="layer",
    )(
        bias_table,
        segments,
        queries,
        key_rows,
        value_rows,
        tokens,
        out_proj,
        router.T,
        jnp.swapaxes(routes_one, 1, 2),
        jnp.swapaxes(routes_two, 1, 2),
        old_table[None],
        new_table[None],
        gate_weight,
        up_weight,
        down_weight,
    )


def solution(mesh):
    placed = (
        P(None, "exp", "seq", None),
        P(None, "exp", "seq", None),
        P(None, "exp", "seq", None),
        P(None, "exp", "seq", None),
        P(None, "exp", "seq"),
        P(),
        P(),
        P(),
        P("exp", None, None),
        P("exp", None, None),
        P("exp", None, None),
        P(),
        P(),
        P("exp", "seq", None),
        P("exp", "seq", None),
    )
    return jax.shard_map(
        local, mesh=mesh, in_specs=placed, out_specs=P(None, "exp", "seq", None), check_vma=False
    )
```

time: 621 us -> 151 us (0.24)
  the two profiles are of different devices: /device:TPU:1 before, /device:TPU:32 now
where the time goes in v2:
time: 151 us
  Pallas kernels  149 us (99%)
  local copies, waits for them, and re-layouts  1.87 us (1%)
    pallas_call x1, Pallas kernels, local(): pl.pallas_call(layer_kernel, out_shape=jax.ShapeDtypeStruct((2, 1, TOK, D...  149 us

profile of v2, /device:TPU:32, one launch (start us, length us, event | category | flops | bytes accessed | tf_op | source)
XLA Modules:
  0.0 150.5 jit_solution(3482452428278936695)
XLA Ops:
  0.0 148.7 %layer.1 = bf16[2,1,128,1024]{3,2,1,0:T(8,128)(2,1)} custom-call(f32[16,32]{1,0:T(8,128)} %bias_hbm.1, s32[2,1,128]{2,1,0:T(1,128)} %seg_hbm.1, bf16[2,1,128,1024]{3,2,1,0:T(8,128)(2,1)} %q_hbm.1, bf16[2,1,128,1024]{3,2,1,0:T(8,128)(2,1)} %k_hbm.1, bf16[2,1,128,1024]{3,2,1,0:T(8,128)(2,1)} %v_hbm.1, bf16[2,1,128,1024]{3,2,1,0:T(8,128)(2,1)} %tok_hbm.1, ...), custom_call_target="tpu_custom_call" | custom-call | tf_op jit(solution)/shard_map/layer/pallas_call | solution.py:675
  148.7 1.9 %copy.17 = bf16[2,1,128,1024]{3,2,1,0:T(8,128)(2,1)} copy(bf16[2,1,128,1024]{3,2,1,0:T(8,128)(2,1)} %layer.1) | data formatting | bytes 1048576

commit v3 on v2

--- a/solution.py
+++ b/solution.py
@@ -137,6 +137,13 @@
     go_recv,
     back_send,
     back_recv,
+    tok_in,
+    place_in,
+    place_out,
+    tok_send,
+    tok_recv,
+    place_send,
+    place_recv,
 ):
     me = lax.axis_index("seq")
     my_exp = lax.axis_index("exp")
@@ -340,6 +347,42 @@
         if batch == 1:
             difference = dot(difference.astype(BF16), serving)
         differences.append(difference)
+    for c in range(2):
+        place_out[c : c + 1, :] = place_rows[1][c]
+    place_in[0] = place_out[...]
+
+    def plane(step):
+        return me_y * EXP_Z + lax.rem(me_z + step, EXP_Z)
+
+    place_copies = [
+        remote(
+            place_out,
+            place_in.at[group],
+            place_send.at[group],
+            place_recv.at[group],
+            exp=plane(step),
+        )
+        for group, step in ((1, 1), (2, 3), (3, 2))
+    ]
+    for copy in place_copies:
+        copy.start()
+
+    def token_copy(group, half):
+        rows = slice(half * (TOK // 2), (half + 1) * (TOK // 2))
+        origin = 1 + half if group == 3 else 0
+        step = (1, 3)[half] if group == 3 else (1, 3)[group - 1]
+        return remote(
+            tok_in.at[origin, rows],
+            tok_in.at[group, rows],
+            tok_send.at[group, half],
+            tok_recv.at[group, half],
+            exp=plane(step),
+        )
+
+    def relay():
+        for half in range(2):
+            token_copy(1 + half, half).wait_recv()
+            token_copy(3, half).start()
 
     lane_head = iota((2 * TOK, LANES), 1) // HALF
     row_head = iota((2 * TOK, LANES), 0) // TOK
@@ -483,6 +526,8 @@
             return carry
 
         lax.fori_loop(0, WIN, attend_late, 0)
+        if not opening:
+            relay()
 
         @pl.when(upper == 1)
         def _():
@@ -495,6 +540,9 @@
         y = lax.rem(me_y + EXP_Y + sign * dy, EXP_Y)
         z = lax.rem(me_z + EXP_Z + sign * plane_step(group), EXP_Z)
         return y * EXP_Z + z
+
+    def beside(dy):
+        return lax.rem(me_y + dy, EXP_Y) * EXP_Z + me_z
 
     def dispatch(batch, group, dy):
         slot = group * EXP_Y + dy
@@ -504,7 +552,7 @@
             rbuf[batch].at[slot, rows],
             go_send.at[batch, slot],
             go_recv.at[batch, slot],
-            exp=target_of(group, dy, 1),
+            exp=beside(dy) if batch == 1 else target_of(group, dy, 1),
         )
 
     def answer(batch, group, dy):
@@ -519,6 +567,29 @@
         )
 
     gates = [None, None]
+
+    def pick(batch, group, places, source):
+        stride = STRIDE[batch]
+        spot = (iota((EXP_Y * stride, TOK), 0) + group * EXP_Y * stride).astype(F32)
+        hit = (spot == places[0]) | (spot == places[1])
+        plan = jnp.where(hit, 1.0, 0.0).astype(BF16)
+        for part in range(2):
+            cols = slice(part * 512, (part + 1) * 512)
+            sbuf[batch][group * EXP_Y : (group + 1) * EXP_Y, :, cols] = (
+                dot(plan, source[:, cols]).astype(BF16).reshape(EXP_Y, stride, 512)
+            )
+
+    def spread(group):
+        if group > 0:
+            place_copies[group - 1].wait_recv()
+            for half in range(2):
+                if (group, half) not in ((1, 0), (2, 1)):
+                    token_copy(group, half).wait_recv()
+        places = [place_in[group, c : c + 1, :] for c in range(2)]
+        pick(1, group, places, tok_in.at[group])
+        for dy in range(1, EXP_Y):
+            dispatch(1, group, dy).start()
+        rbuf[1][group * EXP_Y] = sbuf[1][group * EXP_Y]
 
     def front(batch, opening):
         for step in range(1, PAIRS):
@@ -542,22 +613,23 @@
             )
         value = hidden[batch]
         scale = lax.rsqrt(jnp.mean(value * value, axis=1, keepdims=True) + EPSILON)
-        normed[...] = (value * scale).astype(BF16)
-        stride = STRIDE[batch]
-        for group in (3, 1, 2, 0):
-            spot = (iota((EXP_Y * stride, TOK), 0) + group * EXP_Y * stride).astype(F32)
-            hit = (spot == place_rows[batch][0]) | (spot == place_rows[batch][1])
-            plan = jnp.where(hit, 1.0, 0.0).astype(BF16)
-            for part in range(2):
-                cols = slice(part * 512, (part + 1) * 512)
-                sbuf[batch][group * EXP_Y : (group + 1) * EXP_Y, :, cols] = (
-                    dot(plan, normed[:, cols]).astype(BF16).reshape(EXP_Y, stride, 512)
-                )
-            for dy in range(EXP_Y):
-                if group + dy > 0:
-                    dispatch(batch, group, dy).start()
-        rbuf[batch][0] = sbuf[batch][0]
-        logits = dot_t(normed[...], router[...])
+        rows_value = (value * scale).astype(BF16)
+        if batch == 1:
+            tok_in[0] = rows_value
+            for group, half in ((1, 0), (2, 1), (1, 1), (2, 0)):
+                token_copy(group, half).start()
+            spread(0)
+            source = tok_in[0]
+        else:
+            normed[...] = rows_value
+            for group in (3, 1, 2, 0):
+                pick(batch, group, place_rows[0], normed)
+                for dy in range(EXP_Y):
+                    if group + dy > 0:
+                        dispatch(batch, group, dy).start()
+            rbuf[batch][0] = sbuf[batch][0]
+            source = normed[...]
+        logits = dot_t(source, router[...])
         picked = jnp.sum(differences[batch][:, :N_EXP] * logits, axis=1, keepdims=True)
         first = jax.nn.sigmoid(picked)
         gates[batch] = (first, 1.0 - first)
@@ -568,6 +640,8 @@
 
         def serve(group, carry):
             for dy in range(EXP_Y):
+                if dy == 0 and batch == 1:
+                    continue
                 if dy == 0:
 
                     @pl.when(group > 0)
@@ -623,9 +697,13 @@
             result = result + both[:TOK] + both[TOK:]
         out_ref[batch, 0] = result.astype(BF16)
 
-    for turn, batch in enumerate(ORDER):
-        attention(batch, turn == 0)
-        front(batch, turn == 0)
+    attention(1, True)
+    front(1, True)
+    attention(0, False)
+    spread(1)
+    spread(2)
+    front(0, False)
+    spread(3)
     for copy in late[3:]:
         copy.wait()
     for batch in ORDER:
@@ -636,11 +714,17 @@
     for batch in range(2):
         for group in range(EXP_Z):
             for dy in range(EXP_Y):
+                if dy > 0 or (batch == 0 and group > 0):
+                    dispatch(batch, group, dy).wait_send()
                 if group + dy > 0:
-                    dispatch(batch, group, dy).wait_send()
                     answer(batch, group, dy).wait_send()
         for step in range(1, PAIRS):
             context_copy(batch, lax.rem(pair + step, PAIRS)).wait_send()
+
+    for group in range(1, EXP_Z):
+        place_copies[group - 1].wait_send()
+        for half in range(2):
+            token_copy(group, half).wait_send()
 
     @pl.when(upper == 0)
     def _():
@@ -724,6 +808,13 @@
             dma((2, N_EXP)),
             dma((2, N_EXP)),
             dma((2, N_EXP)),
+            vmem((EXP_Z, TOK, D), BF16),
+            vmem((EXP_Z, 2, TOK), F32),
+            vmem((2, TOK), F32),
+            dma((EXP_Z, 2)),
+            dma((EXP_Z, 2)),
+            dma((EXP_Z,)),
+            dma((EXP_Z,)),
         ],
         compiler_params=pltpu.CompilerParams(
             collective_id=0, has_side_effects=True, vmem_limit_bytes=56 << 20

time: 151 us -> 139 us (0.921)
  Pallas kernels: 149 us -> 136 us
    pallas_call x1, Pallas kernels: 149 us -> 136 us  [local(): pl.pallas_call(layer_kernel, out_shape=jax.ShapeDtypeStruct((2, 1, TOK, D...]
where the time goes in v3:
time: 139 us; the launch traced here: 138 us
  Pallas kernels  136 us (98%)
  local copies, waits for them, and re-layouts  1.87 us (1%)
    pallas_call x1, Pallas kernels, local(): pl.pallas_call(layer_kernel, out_shape=jax.ShapeDtypeStruct((2, 1, TOK, D...  136 us

profile of v3, /device:TPU:32, one launch (start us, length us, event | category | flops | bytes accessed | tf_op | source)
XLA Modules:
  0.0 137.9 jit_solution(14025131392932965224)
XLA Ops:
  0.0 136.0 %layer.1 = bf16[2,1,128,1024]{3,2,1,0:T(8,128)(2,1)} custom-call(f32[16,32]{1,0:T(8,128)} %bias_hbm.1, s32[2,1,128]{2,1,0:T(1,128)} %seg_hbm.1, bf16[2,1,128,1024]{3,2,1,0:T(8,128)(2,1)} %q_hbm.1, bf16[2,1,128,1024]{3,2,1,0:T(8,128)(2,1)} %k_hbm.1, bf16[2,1,128,1024]{3,2,1,0:T(8,128)(2,1)} %v_hbm.1, bf16[2,1,128,1024]{3,2,1,0:T(8,128)(2,1)} %tok_hbm.1, ...), custom_call_target="tpu_custom_call" | custom-call | tf_op jit(solution)/shard_map/layer/pallas_call | solution.py:759
  136.0 1.9 %copy.17 = bf16[2,1,128,1024]{3,2,1,0:T(8,128)(2,1)} copy(bf16[2,1,128,1024]{3,2,1,0:T(8,128)(2,1)} %layer.1) | data formatting | bytes 1048576

commit v4 on v3

--- a/solution.py
+++ b/solution.py
@@ -26,7 +26,6 @@
 STRIDE = (32, 48)
 SENT = (24, 40)
 SINK_BUCKET = 31
-ORDER = (1, 0)
 
 EPSILON = 1e-06
 MASKED = -1e30
@@ -144,6 +143,18 @@
     tok_recv,
     place_send,
     place_recv,
+    gate_in,
+    gate_out,
+    gate_send,
+    gate_recv,
+    part_out,
+    part_in,
+    red_in,
+    part_send,
+    part_recv,
+    red_send,
+    red_recv,
+    hidden_part,
 ):
     me = lax.axis_index("seq")
     my_exp = lax.axis_index("exp")
@@ -282,7 +293,7 @@
 
     for copy in seg_copies:
         copy.start()
-    for copy in qkv[ORDER[0]]:
+    for copy in qkv[1]:
         copy.start()
     for copy in late:
         copy.start()
@@ -366,6 +377,36 @@
     ]
     for copy in place_copies:
         copy.start()
+    gate_copies = [
+        remote(
+            gate_out,
+            gate_in.at[group],
+            gate_send.at[group],
+            gate_recv.at[group],
+            exp=plane(step),
+        )
+        for group, step in ((1, 1), (2, 3), (3, 2))
+    ]
+
+    def part_copy(group, half):
+        rows = slice(half * (TOK // 2), (half + 1) * (TOK // 2))
+        return remote(
+            part_out.at[group, rows],
+            part_in.at[group, rows],
+            part_send.at[group, half],
+            part_recv.at[group, half],
+            exp=plane((3, 1)[group - 1]),
+        )
+
+    def far_copy(half):
+        rows = slice(half * (TOK // 2), (half + 1) * (TOK // 2))
+        return remote(
+            part_out.at[3, rows],
+            red_in.at[half],
+            red_send.at[half],
+            red_recv.at[half],
+            exp=plane((3, 1)[half]),
+        )
 
     def token_copy(group, half):
         rows = slice(half * (TOK // 2), (half + 1) * (TOK // 2))
@@ -424,7 +465,7 @@
                 halo_hop(batch, kind).start()
 
         if opening:
-            for copy in qkv[ORDER[1]]:
+            for copy in qkv[0]:
                 copy.start()
 
             @pl.when(upper == 1)
@@ -563,7 +604,7 @@
             back[batch].at[slot, rows],
             back_send.at[batch, slot],
             back_recv.at[batch, slot],
-            exp=target_of(group, dy, -1),
+            exp=beside(EXP_Y - dy) if batch == 1 else target_of(group, dy, -1),
         )
 
     gates = [None, None]
@@ -633,6 +674,14 @@
         picked = jnp.sum(differences[batch][:, :N_EXP] * logits, axis=1, keepdims=True)
         first = jax.nn.sigmoid(picked)
         gates[batch] = (first, 1.0 - first)
+        if batch == 1:
+            for c in range(2):
+                gate_out[c : c + 1, :] = jnp.transpose(
+                    jnp.broadcast_to(gates[batch][c], (TOK, TOK))
+                )[0:1, :]
+            gate_in[0] = gate_out[...]
+            for copy in gate_copies:
+                copy.start()
 
     def serve_all(batch):
         stride = STRIDE[batch]
@@ -666,7 +715,9 @@
                     .reshape(EXP_Y, stride, 512)
                 )
             for dy in range(EXP_Y):
-                if dy == 0:
+                if dy == 0 and batch == 1:
+                    back[1][group * EXP_Y] = ybuf[1][group * EXP_Y]
+                elif dy == 0:
 
                     @pl.when(group > 0)
                     def _():
@@ -677,25 +728,68 @@
             return carry
 
         lax.fori_loop(0, EXP_Z, serve, 0)
-        back[batch][0] = ybuf[batch][0]
-
-    def combine(batch):
+        if batch == 0:
+            back[batch][0] = ybuf[batch][0]
+
+    def blend(batch, group, places, weights):
         stride = STRIDE[batch]
-        result = hidden[batch]
+        spot = (iota((TOK, EXP_Y * stride), 1) + group * EXP_Y * stride).astype(F32)
+        mix = jnp.where(spot == places[0], weights[0], 0.0) + jnp.where(
+            spot == places[1], weights[1], 0.0
+        )
+        coarse = mix.astype(BF16)
+        fine = (mix - coarse.astype(F32)).astype(BF16)
+        rows = back[batch][group * EXP_Y : (group + 1) * EXP_Y].reshape(EXP_Y * stride, D)
+        both = dot(jnp.concatenate([coarse, fine], axis=0), rows)
+        return both[:TOK] + both[TOK:]
+
+    def plane_sum(group):
+        for dy in range(1, EXP_Y):
+            answer(1, group, dy).wait_recv()
+        if group == 0:
+            return blend(1, 0, place_cols[1], gates[1])
+        gate_copies[group - 1].wait_recv()
+        places = [turned(place_in[group, c : c + 1, :])[:, 0:1] for c in range(2)]
+        weights = [turned(gate_in[group, c : c + 1, :])[:, 0:1] for c in range(2)]
+        return blend(1, group, places, weights)
+
+    half_rows = (slice(0, TOK // 2), slice(TOK // 2, TOK))
+
+    def plane_sums():
+        part_out[3] = plane_sum(3).astype(BF16)
+        for half in range(2):
+            far_copy(half).start()
+        for group in (1, 2):
+            total = plane_sum(group)
+            near, far = half_rows[group - 1], half_rows[2 - group]
+            part_out[group, far] = total[far].astype(BF16)
+            part_copy(group, 2 - group).start()
+            hidden_part[group - 1] = total[near]
+        hidden[1] = hidden[1] + plane_sum(0)
+
+    def pass_on():
+        for group in (1, 2):
+            near = half_rows[group - 1]
+            far_copy(group - 1).wait_recv()
+            total = hidden_part[group - 1] + red_in[group - 1].astype(F32)
+            part_out[group, near] = total.astype(BF16)
+            part_copy(group, group - 1).start()
+
+    def finish_one():
+        result = hidden[0]
         for group in range(EXP_Z):
             for dy in range(EXP_Y):
                 if group + dy > 0:
-                    answer(batch, group, dy).wait_recv()
-            spot = (iota((TOK, EXP_Y * stride), 1) + group * EXP_Y * stride).astype(F32)
-            mix = jnp.where(spot == place_cols[batch][0], gates[batch][0], 0.0) + jnp.where(
-                spot == place_cols[batch][1], gates[batch][1], 0.0
-            )
-            coarse = mix.astype(BF16)
-            fine = (mix - coarse.astype(F32)).astype(BF16)
-            rows = back[batch][group * EXP_Y : (group + 1) * EXP_Y].reshape(EXP_Y * stride, D)
-            both = dot(jnp.concatenate([coarse, fine], axis=0), rows)
-            result = result + both[:TOK] + both[TOK:]
-        out_ref[batch, 0] = result.astype(BF16)
+                    answer(0, group, dy).wait_recv()
+            result = result + blend(0, group, place_cols[0], gates[0])
+        out_ref[0, 0] = result.astype(BF16)
+
+    def finish_two():
+        for group in (1, 2):
+            for half in range(2):
+                part_copy(group, half).wait_recv()
+        result = hidden[1] + part_in[1].astype(F32) + part_in[2].astype(F32)
+        out_ref[1, 0] = result.astype(BF16)
 
     attention(1, True)
     front(1, True)
@@ -706,25 +800,31 @@
     spread(3)
     for copy in late[3:]:
         copy.wait()
-    for batch in ORDER:
-        serve_all(batch)
-    for batch in ORDER:
-        combine(batch)
+    serve_all(1)
+    serve_all(0)
+    plane_sums()
+    pass_on()
+    finish_one()
+    finish_two()
 
     for batch in range(2):
         for group in range(EXP_Z):
             for dy in range(EXP_Y):
                 if dy > 0 or (batch == 0 and group > 0):
                     dispatch(batch, group, dy).wait_send()
-                if group + dy > 0:
                     answer(batch, group, dy).wait_send()
         for step in range(1, PAIRS):
             context_copy(batch, lax.rem(pair + step, PAIRS)).wait_send()
 
     for group in range(1, EXP_Z):
         place_copies[group - 1].wait_send()
+        gate_copies[group - 1].wait_send()
         for half in range(2):
             token_copy(group, half).wait_send()
+            if group < 3:
+                part_copy(group, half).wait_send()
+    for half in range(2):
+        far_copy(half).wait_send()
 
     @pl.when(upper == 0)
     def _():
@@ -815,6 +915,18 @@
             dma((EXP_Z, 2)),
             dma((EXP_Z,)),
             dma((EXP_Z,)),
+            vmem((EXP_Z, 2, TOK), F32),
+            vmem((2, TOK), F32),
+            dma((EXP_Z,)),
+            dma((EXP_Z,)),
+            vmem((EXP_Z, TOK, D), BF16),
+            vmem((EXP_Z, TOK, D), BF16),
+            vmem((2, TOK // 2, D), BF16),
+            dma((EXP_Z, 2)),
+            dma((EXP_Z, 2)),
+            dma((2,)),
+            dma((2,)),
+            vmem((2, TOK // 2, D), F32),
         ],
         compiler_params=pltpu.CompilerParams(
             collective_id=0, has_side_effects=True, vmem_limit_bytes=56 << 20

time: 139 us -> 125 us (0.90)
  Pallas kernels: 136 us -> 121 us
    pallas_call x1, Pallas kernels: 136 us -> 121 us  [local(): pl.pallas_call(layer_kernel, out_shape=jax.ShapeDtypeStruct((2, 1, TOK, D...]
where the time goes in v4:
time: 125 us; the launch traced here: 123 us
  Pallas kernels  121 us (97%)
  local copies, waits for them, and re-layouts  1.87 us (1%)
    pallas_call x1, Pallas kernels, local(): pl.pallas_call(layer_kernel, out_shape=jax.ShapeDtypeStruct((2, 1, TOK, D...  121 us

profile of v4, /device:TPU:32, one launch (start us, length us, event | category | flops | bytes accessed | tf_op | source)
XLA Modules:
  0.0 123.2 jit_solution(18001708601355674465)
XLA Ops:
  0.0 121.3 %layer.1 = bf16[2,1,128,1024]{3,2,1,0:T(8,128)(2,1)} custom-call(f32[16,32]{1,0:T(8,128)} %bias_hbm.1, s32[2,1,128]{2,1,0:T(1,128)} %seg_hbm.1, bf16[2,1,128,1024]{3,2,1,0:T(8,128)(2,1)} %q_hbm.1, bf16[2,1,128,1024]{3,2,1,0:T(8,128)(2,1)} %k_hbm.1, bf16[2,1,128,1024]{3,2,1,0:T(8,128)(2,1)} %v_hbm.1, bf16[2,1,128,1024]{3,2,1,0:T(8,128)(2,1)} %tok_hbm.1, ...), custom_call_target="tpu_custom_call" | custom-call | tf_op jit(solution)/shard_map/layer/pallas_call | solution.py:859
  121.3 1.9 %copy.17 = bf16[2,1,128,1024]{3,2,1,0:T(8,128)(2,1)} copy(bf16[2,1,128,1024]{3,2,1,0:T(8,128)(2,1)} %layer.1) | data formatting | bytes 1048576

commit v5 on v4

--- a/solution.py
+++ b/solution.py
@@ -447,7 +447,7 @@
             ctx_out.at[batch, pair], ctx_in.at[batch, :, lanes_of(pair)], ctx_own.at[batch]
         )
 
-    def attention(batch, opening):
+    def prepare(batch, opening):
         if opening:
             for copy in seg_copies:
                 copy.wait()
@@ -499,12 +499,13 @@
         def _():
             sink_hop(batch).start()
 
+    def attention(batch, opening):
         @pl.when(upper == 1)
         def _():
             sink_hop(batch).wait_recv()
 
-        sink_rows[0] = k_sink + sink_in[batch, 0]
-        sink_rows[1] = v_sink + sink_in[batch, 1]
+        sink_rows[0] = sink_out[batch, 0] + sink_in[batch, 0]
+        sink_rows[1] = sink_out[batch, 1] + sink_in[batch, 1]
 
         def attend(block):
             query = twice(qb[batch, block].astype(F32) * 0.125)
@@ -683,11 +684,12 @@
             for copy in gate_copies:
                 copy.start()
 
-    def serve_all(batch):
+    def serve_all(batch, low, high):
         stride = STRIDE[batch]
         count = EXP_Y * stride
 
-        def serve(group, carry):
+        def serve(turn, carry):
+            group = lax.rem(turn + 1, EXP_Z)
             for dy in range(EXP_Y):
                 if dy == 0 and batch == 1:
                     continue
@@ -727,8 +729,8 @@
                     answer(batch, group, dy).start()
             return carry
 
-        lax.fori_loop(0, EXP_Z, serve, 0)
-        if batch == 0:
+        lax.fori_loop(low, high, serve, 0)
+        if batch == 0 and high == EXP_Z:
             back[batch][0] = ybuf[batch][0]
 
     def blend(batch, group, places, weights):
@@ -765,7 +767,6 @@
             part_out[group, far] = total[far].astype(BF16)
             part_copy(group, 2 - group).start()
             hidden_part[group - 1] = total[near]
-        hidden[1] = hidden[1] + plane_sum(0)
 
     def pass_on():
         for group in (1, 2):
@@ -785,13 +786,16 @@
         out_ref[0, 0] = result.astype(BF16)
 
     def finish_two():
+        result = hidden[1] + plane_sum(0)
         for group in (1, 2):
             for half in range(2):
                 part_copy(group, half).wait_recv()
-        result = hidden[1] + part_in[1].astype(F32) + part_in[2].astype(F32)
+        result = result + part_in[1].astype(F32) + part_in[2].astype(F32)
         out_ref[1, 0] = result.astype(BF16)
 
+    prepare(1, True)
     attention(1, True)
+    prepare(0, False)
     front(1, True)
     attention(0, False)
     spread(1)
@@ -800,10 +804,11 @@
     spread(3)
     for copy in late[3:]:
         copy.wait()
-    serve_all(1)
-    serve_all(0)
+    serve_all(1, 0, EXP_Z)
     plane_sums()
+    serve_all(0, 0, 2)
     pass_on()
+    serve_all(0, 2, EXP_Z)
     finish_one()
     finish_two()
 

time: 125 us -> 125 us (level); the launches traced: 123 us -> 125 us
  Pallas kernels: 121 us -> 123 us
    pallas_call x1, Pallas kernels: 121 us -> 123 us  [local(): pl.pallas_call(layer_kernel, out_shape=jax.ShapeDtypeStruct((2, 1, TOK, D...]
where the time goes in v5:
time: 125 us
  Pallas kernels  123 us (98%)
  local copies, waits for them, and re-layouts  1.87 us (1%)
    pallas_call x1, Pallas kernels, local(): pl.pallas_call(layer_kernel, out_shape=jax.ShapeDtypeStruct((2, 1, TOK, D...  123 us

profile of v5, /device:TPU:32, one launch (start us, length us, event | category | flops | bytes accessed | tf_op | source)
XLA Modules:
  0.0 125.3 jit_solution(2568290037062534691)
XLA Ops:
  0.0 123.4 %layer.1 = bf16[2,1,128,1024]{3,2,1,0:T(8,128)(2,1)} custom-call(f32[16,32]{1,0:T(8,128)} %bias_hbm.1, s32[2,1,128]{2,1,0:T(1,128)} %seg_hbm.1, bf16[2,1,128,1024]{3,2,1,0:T(8,128)(2,1)} %q_hbm.1, bf16[2,1,128,1024]{3,2,1,0:T(8,128)(2,1)} %k_hbm.1, bf16[2,1,128,1024]{3,2,1,0:T(8,128)(2,1)} %v_hbm.1, bf16[2,1,128,1024]{3,2,1,0:T(8,128)(2,1)} %tok_hbm.1, ...), custom_call_target="tpu_custom_call" | custom-call | tf_op jit(solution)/shard_map/layer/pallas_call | solution.py:864
  123.4 1.9 %copy.17 = bf16[2,1,128,1024]{3,2,1,0:T(8,128)(2,1)} copy(bf16[2,1,128,1024]{3,2,1,0:T(8,128)(2,1)} %layer.1) | data formatting | bytes 1048576

commit v6 on v5

--- a/solution.py
+++ b/solution.py
@@ -447,15 +447,32 @@
             ctx_out.at[batch, pair], ctx_in.at[batch, :, lanes_of(pair)], ctx_own.at[batch]
         )
 
+    def columns(batch):
+        def column(block, before):
+            line = segs[batch, block]
+            segcol[batch, block] = turned(line)
+            document = iota((8, TOK), 0)
+            return before + jnp.where((line < document) & (line >= 0), 1, 0)
+
+        ahead = lax.fori_loop(
+            0, 2 * PAIRS, column, jnp.zeros((8, TOK), I32), unroll=4
+        )
+        return jnp.sum(ahead, axis=1, keepdims=True)
+
+    for copy in seg_copies:
+        copy.wait()
+
+    @pl.when(upper == 0)
+    def _():
+        seg_hop.start()
+
+    @pl.when(upper == 1)
+    def _():
+        seg_hop.wait_recv()
+
+    starts = [columns(batch) for batch in range(2)]
+
     def prepare(batch, opening):
-        if opening:
-            for copy in seg_copies:
-                copy.wait()
-
-            @pl.when(upper == 0)
-            def _():
-                seg_hop.start()
-
         for copy in qkv[batch]:
             copy.wait()
 
@@ -468,30 +485,17 @@
             for copy in qkv[0]:
                 copy.start()
 
-            @pl.when(upper == 1)
-            def _():
-                seg_hop.wait_recv()
-
-        def columns(block, before):
-            line = segs[batch, block]
-            segcol[block] = turned(line)
-            document = iota((8, TOK), 0)
-            return before + jnp.where((line < document) & (line >= 0), 1, 0)
-
-        ahead = lax.fori_loop(0, 2 * PAIRS, columns, jnp.zeros((8, TOK), I32))
-        starts = jnp.sum(ahead, axis=1, keepdims=True)
-
         def sinks(block, sums):
             k_sum, v_sum = sums
             spot = (upper * PAIRS + block) * TOK + iota((8, TOK), 1)
-            pick = jnp.where(spot == starts, 1.0, 0.0).astype(BF16)
+            pick = jnp.where(spot == starts[batch], 1.0, 0.0).astype(BF16)
             return (
                 k_sum + dot(pick, kb[batch, block + WIN]),
                 v_sum + dot(pick, vb[batch, block + WIN]),
             )
 
         zero = jnp.zeros((8, LANES), F32)
-        k_sink, v_sink = lax.fori_loop(0, PAIRS, sinks, (zero, zero))
+        k_sink, v_sink = lax.fori_loop(0, PAIRS, sinks, (zero, zero), unroll=True)
         sink_out[batch, 0] = k_sink
         sink_out[batch, 1] = v_sink
 
@@ -511,7 +515,7 @@
             query = twice(qb[batch, block].astype(F32) * 0.125)
             query = jnp.where(own_half, query, 0.0)
             query_rows = query.astype(BF16)
-            mine = segcol[block + PAIRS]
+            mine = segcol[batch, block + PAIRS]
             pieces = []
             for near in range(WIN + 1):
                 raw = dot_t(query_rows, kb[batch, block + near])
@@ -528,7 +532,7 @@
             chosen_doc = iota((8, LANES), 0) == segs[batch, block + PAIRS][:, 0:1]
             k_row = jnp.sum(jnp.where(chosen_doc, sink_rows[0], 0.0), axis=0, keepdims=True)
             v_row = jnp.sum(jnp.where(chosen_doc, sink_rows[1], 0.0), axis=0, keepdims=True)
-            sink_seen = twice(mine[:, 0:1] == segcol[block + WIN][:, 0:1])
+            sink_seen = twice(mine[:, 0:1] == segcol[batch, block + WIN][:, 0:1])
             sink = jnp.sum(query * k_row, axis=1, keepdims=True) + sink_bias
             sink = jnp.where(sink_seen, sink, MASKED)
             peak = jnp.maximum(
@@ -567,7 +571,7 @@
             attend(lax.rem(pair + turn, WIN))
             return carry
 
-        lax.fori_loop(0, WIN, attend_late, 0)
+        lax.fori_loop(0, WIN, attend_late, 0, unroll=2)
         if not opening:
             relay()
 
@@ -576,7 +580,7 @@
             for kind in range(2):
                 halo_hop(batch, kind).wait_recv()
 
-        lax.fori_loop(0, WIN, attend_early, 0)
+        lax.fori_loop(0, WIN, attend_early, 0, unroll=2)
 
     def target_of(group, dy, sign):
         y = lax.rem(me_y + EXP_Y + sign * dy, EXP_Y)
@@ -684,24 +688,26 @@
             for copy in gate_copies:
                 copy.start()
 
-    def serve_all(batch, low, high):
-        stride = STRIDE[batch]
-        count = EXP_Y * stride
+    def serve_all(batch, first, last):
+        sent = SENT[batch]
+        slots = 2 * EXP_Y
+        count = slots * sent
 
         def serve(turn, carry):
-            group = lax.rem(turn + 1, EXP_Z)
-            for dy in range(EXP_Y):
-                if dy == 0 and batch == 1:
-                    continue
-                if dy == 0:
+            pair_of_groups = 1 - turn
+            spots = pl.ds(pair_of_groups * slots, slots)
+            for which in range(slots):
+                group, dy = 2 * pair_of_groups + which // EXP_Y, which % EXP_Y
+                if dy > 0:
+                    dispatch(batch, group, dy).wait_recv()
+                elif batch == 0:
 
                     @pl.when(group > 0)
                     def _():
                         dispatch(batch, group, dy).wait_recv()
 
-                else:
-                    dispatch(batch, group, dy).wait_recv()
-            inputs = rbuf[batch][pl.ds(group * EXP_Y, EXP_Y)].reshape(count, D)
+            inputs = rbuf[batch][spots, 0:sent, :].astype(F32)
+            inputs = inputs.reshape(count, D).astype(BF16)
             for low, high in ((0, 512), (512, 1024), (1024, FFW)):
                 gate = dot(inputs, gate_w[:, low:high])
                 up = dot(inputs, up_w[:, low:high])
@@ -711,27 +717,26 @@
                 )
             for part in range(2):
                 cols = slice(part * 512, (part + 1) * 512)
-                ybuf[batch][pl.ds(group * EXP_Y, EXP_Y), :, cols] = (
-                    dot(active[0:count], down_w[:, cols])
-                    .astype(BF16)
-                    .reshape(EXP_Y, stride, 512)
+                ybuf[batch][spots, 0:sent, cols] = (
+                    dot(active[0:count], down_w[:, cols]).reshape(slots, sent, 512).astype(BF16)
                 )
-            for dy in range(EXP_Y):
-                if dy == 0 and batch == 1:
-                    back[1][group * EXP_Y] = ybuf[1][group * EXP_Y]
-                elif dy == 0:
+            for which in range(slots):
+                group, dy = 2 * pair_of_groups + which // EXP_Y, which % EXP_Y
+                if dy > 0:
+                    answer(batch, group, dy).start()
+                elif batch == 1:
+                    back[1][group * EXP_Y, 0:sent] = ybuf[1][group * EXP_Y, 0:sent]
+                else:
 
                     @pl.when(group > 0)
                     def _():
                         answer(batch, group, dy).start()
 
-                else:
-                    answer(batch, group, dy).start()
             return carry
 
-        lax.fori_loop(low, high, serve, 0)
-        if batch == 0 and high == EXP_Z:
-            back[batch][0] = ybuf[batch][0]
+        lax.fori_loop(first, last, serve, 0)
+        if batch == 0 and last == 2:
+            back[batch][0, 0:sent] = ybuf[batch][0, 0:sent]
 
     def blend(batch, group, places, weights):
         stride = STRIDE[batch]
@@ -798,17 +803,17 @@
     prepare(0, False)
     front(1, True)
     attention(0, False)
+    front(0, False)
     spread(1)
     spread(2)
-    front(0, False)
     spread(3)
     for copy in late[3:]:
         copy.wait()
-    serve_all(1, 0, EXP_Z)
+    serve_all(1, 0, 2)
     plane_sums()
-    serve_all(0, 0, 2)
+    serve_all(0, 0, 1)
     pass_on()
-    serve_all(0, 2, EXP_Z)
+    serve_all(0, 1, 2)
     finish_one()
     finish_two()
 
@@ -881,7 +886,7 @@
             vmem((2, PAIRS, TOK, LANES), BF16),
             vmem((2, PAIRS + WIN, TOK, LANES), BF16),
             vmem((2, PAIRS + WIN, TOK, LANES), BF16),
-            vmem((N_SEQ, TOK, TOK), I32),
+            vmem((2, N_SEQ, TOK, TOK), I32),
             vmem((WIN, 2 * TOK, TOK), F32),
             vmem((2, 2, 8, LANES), F32),
             vmem((2, 2, 8, LANES), F32),
@@ -894,7 +899,7 @@
             *buffers,
             *buffers,
             *buffers,
-            vmem((EXP_Y * STRIDE[1], FFW), BF16),
+            vmem((2 * EXP_Y * SENT[1], FFW), BF16),
             dma((11,)),
             dma((2, 3, PAIRS)),
             dma((2, 3, PAIRS)),

time: 125 us -> 137 us (1.096)
  the two profiles are of different devices: /device:TPU:32 before, /device:TPU:35 now
where the time goes in v6:
time: 137 us; the launch traced here: 136 us
  Pallas kernels  135 us (99%)
  local copies, waits for them, and re-layouts  1.87 us (1%)
    pallas_call x1, Pallas kernels, local(): pl.pallas_call(layer_kernel, out_shape=jax.ShapeDtypeStruct((2, 1, TOK, D...  135 us

profile of v6, /device:TPU:35, one launch (start us, length us, event | category | flops | bytes accessed | tf_op | source)
XLA Modules:
  0.0 136.4 jit_solution(5149570369475051710)
XLA Ops:
  0.0 134.6 %layer.1 = bf16[2,1,128,1024]{3,2,1,0:T(8,128)(2,1)} custom-call(f32[16,32]{1,0:T(8,128)} %bias_hbm.1, s32[2,1,128]{2,1,0:T(1,128)} %seg_hbm.1, bf16[2,1,128,1024]{3,2,1,0:T(8,128)(2,1)} %q_hbm.1, bf16[2,1,128,1024]{3,2,1,0:T(8,128)(2,1)} %k_hbm.1, bf16[2,1,128,1024]{3,2,1,0:T(8,128)(2,1)} %v_hbm.1, bf16[2,1,128,1024]{3,2,1,0:T(8,128)(2,1)} %tok_hbm.1, ...), custom_call_target="tpu_custom_call" | custom-call | tf_op jit(solution)/shard_map/layer/pallas_call | solution.py:869
  134.6 1.9 %copy.17 = bf16[2,1,128,1024]{3,2,1,0:T(8,128)(2,1)} copy(bf16[2,1,128,1024]{3,2,1,0:T(8,128)(2,1)} %layer.1) | data formatting | bytes 1048576

commit v7 on v5

--- a/solution.py
+++ b/solution.py
@@ -23,8 +23,10 @@
 LANES = 128
 HALF = 64
 CAP = 20
-STRIDE = (32, 48)
-SENT = (24, 40)
+STRIDE = (48, 48)
+SENT = (40, 40)
+WIDTH = (512, 1024)
+PACK = 32
 SINK_BUCKET = 31
 
 EPSILON = 1e-06
@@ -195,7 +197,8 @@
 
     for batch in range(2):
         low = STRIDE[batch] - 16
-        back[batch][:, low:, :] = jnp.zeros((N_EXP, 16, D), BF16)
+        back[batch][:, low:, :] = jnp.zeros((N_EXP, 16, WIDTH[batch]), BF16)
+    rbuf[0][:, STRIDE[0] - 16 :, :] = jnp.zeros((N_EXP, 16, WIDTH[0]), BF16)
 
     @pl.when(upper == 0)
     def _():
@@ -615,6 +618,14 @@
         spot = (iota((EXP_Y * stride, TOK), 0) + group * EXP_Y * stride).astype(F32)
         hit = (spot == places[0]) | (spot == places[1])
         plan = jnp.where(hit, 1.0, 0.0).astype(BF16)
+        if batch == 0:
+            hit = (spot == places[0] + CAP) | (spot == places[1] + CAP)
+            other = jnp.where(hit, 1.0, 0.0).astype(BF16)
+            halves = dot(plan, source[:, : WIDTH[0]]) + dot(other, source[:, WIDTH[0] :])
+            sbuf[0][group * EXP_Y : (group + 1) * EXP_Y] = halves.astype(BF16).reshape(
+                EXP_Y, stride, WIDTH[0]
+            )
+            return
         for part in range(2):
             cols = slice(part * 512, (part + 1) * 512)
             sbuf[batch][group * EXP_Y : (group + 1) * EXP_Y, :, cols] = (
@@ -686,7 +697,23 @@
 
     def serve_all(batch, low, high):
         stride = STRIDE[batch]
-        count = EXP_Y * stride
+        count = EXP_Y * (stride if batch == 1 else PACK)
+        if batch == 0:
+            inner_row = iota((PACK, EXP_Y * stride), 0)
+            inner_col = iota((PACK, EXP_Y * stride), 1)
+            outer_row = iota((stride, EXP_Y * PACK), 0)
+            outer_col = iota((stride, EXP_Y * PACK), 1)
+            unpack, pack = [], []
+            for side in range(2):
+                near, far = [], []
+                for dy in range(EXP_Y):
+                    hit = inner_col == inner_row + (dy * stride + side * CAP)
+                    near.append(jnp.where(hit & (inner_row < CAP), 1.0, 0.0))
+                    hit = outer_col == outer_row + (dy * PACK - side * CAP)
+                    inside = (outer_row >= side * CAP) & (outer_row < (side + 1) * CAP)
+                    far.append(jnp.where(hit & inside, 1.0, 0.0))
+                unpack.append(jnp.concatenate(near, axis=0).astype(BF16))
+                pack.append(jnp.concatenate(far, axis=0).astype(BF16))
 
         def serve(turn, carry):
             group = lax.rem(turn + 1, EXP_Z)
@@ -701,7 +728,15 @@
 
                 else:
                     dispatch(batch, group, dy).wait_recv()
-            inputs = rbuf[batch][pl.ds(group * EXP_Y, EXP_Y)].reshape(count, D)
+            arrived = rbuf[batch][pl.ds(group * EXP_Y, EXP_Y)].reshape(
+                EXP_Y * stride, WIDTH[batch]
+            )
+            if batch == 0:
+                inputs = jnp.concatenate(
+                    [dot(unpack[side], arrived).astype(BF16) for side in range(2)], axis=1
+                )
+            else:
+                inputs = arrived
             for low, high in ((0, 512), (512, 1024), (1024, FFW)):
                 gate = dot(inputs, gate_w[:, low:high])
                 up = dot(inputs, up_w[:, low:high])
@@ -709,7 +744,16 @@
                 active[0:count, low:high] = (0.5 * gate * (1.0 + jnp.tanh(inner)) * up).astype(
                     BF16
                 )
-            for part in range(2):
+            if batch == 0:
+                outs = [
+                    dot(active[0:count], down_w[:, side * 512 : (side + 1) * 512]).astype(BF16)
+                    for side in range(2)
+                ]
+                halves = dot(pack[0], outs[0]) + dot(pack[1], outs[1])
+                ybuf[0][pl.ds(group * EXP_Y, EXP_Y)] = halves.astype(BF16).reshape(
+                    EXP_Y, stride, WIDTH[0]
+                )
+            for part in range(2 * batch):
                 cols = slice(part * 512, (part + 1) * 512)
                 ybuf[batch][pl.ds(group * EXP_Y, EXP_Y), :, cols] = (
                     dot(active[0:count], down_w[:, cols])
@@ -736,14 +780,24 @@
     def blend(batch, group, places, weights):
         stride = STRIDE[batch]
         spot = (iota((TOK, EXP_Y * stride), 1) + group * EXP_Y * stride).astype(F32)
-        mix = jnp.where(spot == places[0], weights[0], 0.0) + jnp.where(
-            spot == places[1], weights[1], 0.0
-        )
-        coarse = mix.astype(BF16)
-        fine = (mix - coarse.astype(F32)).astype(BF16)
-        rows = back[batch][group * EXP_Y : (group + 1) * EXP_Y].reshape(EXP_Y * stride, D)
-        both = dot(jnp.concatenate([coarse, fine], axis=0), rows)
-        return both[:TOK] + both[TOK:]
+        shifts = (0, CAP) if batch == 0 else (0,)
+        terms = []
+        for shift in shifts:
+            mix = jnp.where(spot == places[0] + shift, weights[0], 0.0) + jnp.where(
+                spot == places[1] + shift, weights[1], 0.0
+            )
+            coarse = mix.astype(BF16)
+            terms += [coarse, (mix - coarse.astype(F32)).astype(BF16)]
+        rows = back[batch][group * EXP_Y : (group + 1) * EXP_Y].reshape(
+            EXP_Y * stride, WIDTH[batch]
+        )
+        both = dot(jnp.concatenate(terms, axis=0), rows)
+        sums = [
+            both[2 * side * TOK : (2 * side + 1) * TOK]
+            + both[(2 * side + 1) * TOK : (2 * side + 2) * TOK]
+            for side in range(len(shifts))
+        ]
+        return sums[0] if batch == 1 else jnp.concatenate(sums, axis=1)
 
     def plane_sum(group):
         for dy in range(1, EXP_Y):
@@ -860,7 +914,7 @@
     any_spec = pl.BlockSpec(memory_space=pl.ANY)
     vmem = pltpu.VMEM
     dma = pltpu.SemaphoreType.DMA
-    buffers = [vmem((N_EXP, stride, D), BF16) for stride in STRIDE]
+    buffers = [vmem((N_EXP, stride, width), BF16) for stride, width in zip(STRIDE, WIDTH)]
     return pl.pallas_call(
         layer_kernel,
         out_shape=jax.ShapeDtypeStruct((2, 1, TOK, D), BF16),

time: 125 us -> 121 us (0.968)
  Pallas kernels: 123 us -> 119 us
    pallas_call x1, Pallas kernels: 123 us -> 119 us  [local(): pl.pallas_call(layer_kernel, out_shape=jax.ShapeDtypeStruct((2, 1, TOK, D...]
where the time goes in v7:
time: 121 us
  Pallas kernels  119 us (98%)
  local copies, waits for them, and re-layouts  1.87 us (2%)
    pallas_call x1, Pallas kernels, local(): pl.pallas_call(layer_kernel, out_shape=jax.ShapeDtypeStruct((2, 1, TOK, D...  119 us

profile of v7, /device:TPU:32, one launch (start us, length us, event | category | flops | bytes accessed | tf_op | source)
XLA Modules:
  0.0 121.0 jit_solution(8548798857278019569)
XLA Ops:
  0.0 119.1 %layer.1 = bf16[2,1,128,1024]{3,2,1,0:T(8,128)(2,1)} custom-call(f32[16,32]{1,0:T(8,128)} %bias_hbm.1, s32[2,1,128]{2,1,0:T(1,128)} %seg_hbm.1, bf16[2,1,128,1024]{3,2,1,0:T(8,128)(2,1)} %q_hbm.1, bf16[2,1,128,1024]{3,2,1,0:T(8,128)(2,1)} %k_hbm.1, bf16[2,1,128,1024]{3,2,1,0:T(8,128)(2,1)} %v_hbm.1, bf16[2,1,128,1024]{3,2,1,0:T(8,128)(2,1)} %tok_hbm.1, ...), custom_call_target="tpu_custom_call" | custom-call | tf_op jit(solution)/shard_map/layer/pallas_call | solution.py:918
  119.1 1.9 %copy.17 = bf16[2,1,128,1024]{3,2,1,0:T(8,128)(2,1)} copy(bf16[2,1,128,1024]{3,2,1,0:T(8,128)(2,1)} %layer.1) | data formatting | bytes 1048576

commit v8 on v7

--- a/solution.py
+++ b/solution.py
@@ -475,6 +475,7 @@
             def _():
                 seg_hop.wait_recv()
 
+    def find_starts(batch):
         def columns(block, before):
             line = segs[batch, block]
             segcol[block] = turned(line)
@@ -669,8 +670,10 @@
         rows_value = (value * scale).astype(BF16)
         if batch == 1:
             tok_in[0] = rows_value
+            prepare(0, False)
             for group, half in ((1, 0), (2, 1), (1, 1), (2, 0)):
                 token_copy(group, half).start()
+            find_starts(0)
             spread(0)
             source = tok_in[0]
         else:
@@ -848,8 +851,8 @@
         out_ref[1, 0] = result.astype(BF16)
 
     prepare(1, True)
+    find_starts(1)
     attention(1, True)
-    prepare(0, False)
     front(1, True)
     attention(0, False)
     spread(1)

time: 121 us -> 130 us (1.074)
  Pallas kernels: 119 us -> 128 us
    pallas_call x1, Pallas kernels: 119 us -> 128 us  [local(): pl.pallas_call(layer_kernel, out_shape=jax.ShapeDtypeStruct((2, 1, TOK, D...]
where the time goes in v8:
time: 130 us; the launch traced here: 129 us
  Pallas kernels  128 us (98%)
  local copies, waits for them, and re-layouts  1.87 us (1%)
    pallas_call x1, Pallas kernels, local(): pl.pallas_call(layer_kernel, out_shape=jax.ShapeDtypeStruct((2, 1, TOK, D...  128 us

profile of v8, /device:TPU:32, one launch (start us, length us, event | category | flops | bytes accessed | tf_op | source)
XLA Modules:
  0.0 129.5 jit_solution(320692179327386391)
XLA Ops:
  0.0 127.6 %layer.1 = bf16[2,1,128,1024]{3,2,1,0:T(8,128)(2,1)} custom-call(f32[16,32]{1,0:T(8,128)} %bias_hbm.1, s32[2,1,128]{2,1,0:T(1,128)} %seg_hbm.1, bf16[2,1,128,1024]{3,2,1,0:T(8,128)(2,1)} %q_hbm.1, bf16[2,1,128,1024]{3,2,1,0:T(8,128)(2,1)} %k_hbm.1, bf16[2,1,128,1024]{3,2,1,0:T(8,128)(2,1)} %v_hbm.1, bf16[2,1,128,1024]{3,2,1,0:T(8,128)(2,1)} %tok_hbm.1, ...), custom_call_target="tpu_custom_call" | custom-call | tf_op jit(solution)/shard_map/layer/pallas_call | solution.py:921
  127.6 1.9 %copy.17 = bf16[2,1,128,1024]{3,2,1,0:T(8,128)(2,1)} copy(bf16[2,1,128,1024]{3,2,1,0:T(8,128)(2,1)} %layer.1) | data formatting | bytes 1048576

commit v9 on v8

--- a/solution.py
+++ b/solution.py
@@ -671,9 +671,9 @@
         if batch == 1:
             tok_in[0] = rows_value
             prepare(0, False)
+            find_starts(0)
             for group, half in ((1, 0), (2, 1), (1, 1), (2, 0)):
                 token_copy(group, half).start()
-            find_starts(0)
             spread(0)
             source = tok_in[0]
         else:

time: 130 us -> 128 us (0.985)
  the two profiles are of different devices: /device:TPU:32 before, /device:TPU:6 now
where the time goes in v9:
time: 128 us
  Pallas kernels  126 us (98%)
  local copies, waits for them, and re-layouts  1.87 us (1%)
    pallas_call x1, Pallas kernels, local(): pl.pallas_call(layer_kernel, out_shape=jax.ShapeDtypeStruct((2, 1, TOK, D...  126 us

profile of v9, /device:TPU:6, one launch (start us, length us, event | category | flops | bytes accessed | tf_op | source)
XLA Modules:
  0.0 127.6 jit_solution(14250303717970756398)
XLA Ops:
  0.0 125.7 %layer.1 = bf16[2,1,128,1024]{3,2,1,0:T(8,128)(2,1)} custom-call(f32[16,32]{1,0:T(8,128)} %bias_hbm.1, s32[2,1,128]{2,1,0:T(1,128)} %seg_hbm.1, bf16[2,1,128,1024]{3,2,1,0:T(8,128)(2,1)} %q_hbm.1, bf16[2,1,128,1024]{3,2,1,0:T(8,128)(2,1)} %k_hbm.1, bf16[2,1,128,1024]{3,2,1,0:T(8,128)(2,1)} %v_hbm.1, bf16[2,1,128,1024]{3,2,1,0:T(8,128)(2,1)} %tok_hbm.1, ...), custom_call_target="tpu_custom_call" | custom-call | tf_op jit(solution)/shard_map/layer/pallas_call | solution.py:921
  125.7 1.9 %copy.17 = bf16[2,1,128,1024]{3,2,1,0:T(8,128)(2,1)} copy(bf16[2,1,128,1024]{3,2,1,0:T(8,128)(2,1)} %layer.1) | data formatting | bytes 1048576

commit v10 on v7

--- a/solution.py
+++ b/solution.py
@@ -459,7 +459,13 @@
             def _():
                 seg_hop.start()
 
-        for copy in qkv[batch]:
+        soon = 12 if opening else 0
+        for copy in qkv[batch][:soon]:
+            copy.wait()
+        if opening:
+            for copy in qkv[0]:
+                copy.start()
+        for copy in qkv[batch][soon:]:
             copy.wait()
 
         @pl.when(upper == 0)
@@ -468,8 +474,6 @@
                 halo_hop(batch, kind).start()
 
         if opening:
-            for copy in qkv[0]:
-                copy.start()
 
             @pl.when(upper == 1)
             def _():

time: 121 us -> 122 us (level); the launches traced: 121 us -> 121 us
  no operation moved by 1% of the time
where the time goes in v10:
time: 122 us; the launch traced here: 121 us
  Pallas kernels  119 us (98%)
  local copies, waits for them, and re-layouts  1.87 us (2%)
    pallas_call x1, Pallas kernels, local(): pl.pallas_call(layer_kernel, out_shape=jax.ShapeDtypeStruct((2, 1, TOK, D...  119 us

profile of v10, /device:TPU:32, one launch (start us, length us, event | category | flops | bytes accessed | tf_op | source)
XLA Modules:
  0.0 120.7 jit_solution(14631023294816413258)
XLA Ops:
  0.0 118.8 %layer.1 = bf16[2,1,128,1024]{3,2,1,0:T(8,128)(2,1)} custom-call(f32[16,32]{1,0:T(8,128)} %bias_hbm.1, s32[2,1,128]{2,1,0:T(1,128)} %seg_hbm.1, bf16[2,1,128,1024]{3,2,1,0:T(8,128)(2,1)} %q_hbm.1, bf16[2,1,128,1024]{3,2,1,0:T(8,128)(2,1)} %k_hbm.1, bf16[2,1,128,1024]{3,2,1,0:T(8,128)(2,1)} %v_hbm.1, bf16[2,1,128,1024]{3,2,1,0:T(8,128)(2,1)} %tok_hbm.1, ...), custom_call_target="tpu_custom_call" | custom-call | tf_op jit(solution)/shard_map/layer/pallas_call | solution.py:922
  118.8 1.9 %copy.17 = bf16[2,1,128,1024]{3,2,1,0:T(8,128)(2,1)} copy(bf16[2,1,128,1024]{3,2,1,0:T(8,128)(2,1)} %layer.1) | data formatting | bytes 1048576
